TPU v7x, 512 devices: a whole 4x8x8 slice. The times are simulated.
512 devices in a mesh: sta: 64 (over y, x, z_hi), win: 8 (over z_lo, core).
Axes of the slice: x: 4, y: 8, z: 8 (z_hi: 2, z_lo: 4; z = z_hi * 4 + z_lo), core: 2. Of those that a mesh axis runs over, the one named last changes fastest.
Arguments:
- spectra: float32 [16, 256, 2, 3, 1664], P('win', 'sta')
- flags: int32 [16, 256], P('win', 'sta'), may hold values 0 or 1
- owners: int32 [4], replicated, may hold values from 0 to 63, as said below
- source_slots: int32 [4, 4], replicated, may hold values from 0 to 3, as said below
Outputs:
- correlations: float32 [4, 4, 3, 256, 3, 768], P(None, None, None, 'sta')
Inputs may be any that keep to these rules, and one draw needn't show every extreme that they name: `owners`: the index of a block of 4 stations along sta. `source_slots`: distinct within a step.
All inputs are finite; a program needn't handle non-finite values. No bound on the sum of `flags` on one device may be relied on, other than what follows from the above.
Results may differ from a plain program's by a relative error of at most 0.0037.
Values sent between devices are 32-bit elements; how exact they have to be, the bound alone decides.
A program may use at most 64 MiB of HBM per device.

v0:
```python
import math

import jax
import jax.numpy as jnp
from jax import lax
from jax.experimental import pallas as pl
from jax.experimental.pallas import tpu as pltpu
from jax.sharding import Mesh
from jax.sharding import PartitionSpec as P

NLAG = 768
STEPS = 4
STA = ("y", "x", "zh")
WIN = ("zl", "c")


def fine_mesh(mesh):
    devs = mesh.devices
    n_sta, n_win = devs.shape
    col = devs[:, 0]
    ny = len({d.coords[1] for d in col})
    nx = len({d.coords[0] for d in col})
    nzh = n_sta // (ny * nx)
    nc = len({d.core_on_chip for d in devs[0, :]})
    nzl = n_win // nc
    return Mesh(devs.reshape(ny, nx, nzh, nzl, nc), STA + WIN)


def a2a_sum(x, axes, n):
    parts = lax.all_to_all(x.reshape(n, -1), axes, 0, 0, tiled=True)
    return jnp.sum(parts.reshape(n, -1), axis=0)


def a2a_gather(x, axes, n):
    return lax.all_to_all(jnp.broadcast_to(x[None], (n, x.shape[0])), axes, 0, 0, tiled=True)


def broadcast_owner(masked):
    plane = ("y", "x")
    n = lax.axis_size(plane)
    piece = a2a_sum(masked, plane, n)
    piece = piece + lax.ppermute(piece, "zh", [(0, 1), (1, 0)])
    return a2a_gather(piece, plane, n).reshape(masked.shape)


def sum_over(x, axis, inner):
    n = lax.axis_size(axis)
    part = a2a_sum(x, axis, n)
    if inner is not None:
        part = sum_over_inner(part, inner)
    return a2a_gather(part, axis, n).reshape(x.shape)


def sum_over_inner(x, axis):
    n = lax.axis_size(axis)
    part = a2a_sum(x, axis, n)
    return a2a_gather(part, axis, n).reshape(x.shape)


def whiten(spectra):
    shape = spectra.shape
    blocks = spectra.reshape(shape[0], shape[1], 2, 3, shape[4] // 64, 64)
    power = jnp.mean(blocks * blocks, axis=(2, 3, 5), keepdims=True)
    return (blocks / jnp.sqrt(power + 1e-06)).reshape(shape)


def lag_table_fast(bins, lags, windows):
    freq = jnp.arange(bins, dtype=jnp.int32) + 360
    q = jnp.arange(lags // 128, dtype=jnp.int32) * 128 - lags // 2
    k = jnp.arange(128, dtype=jnp.int32)
    unit = 2.0 * math.pi / 7200.0
    a = jnp.mod(freq[:, None] * q[None, :], 7200).astype(jnp.float32) * unit
    b = jnp.mod(freq[:, None] * k[None, :], 7200).astype(jnp.float32) * unit
    ca, sa = jnp.cos(a)[:, :, None], jnp.sin(a)[:, :, None]
    cb, sb = jnp.cos(b)[:, None, :], jnp.sin(b)[:, None, :]
    scale = 1.0 / math.sqrt(windows * bins)
    cos = ((ca * cb - sa * sb) * scale).reshape(bins, lags)
    sin = ((sa * cb + ca * sb) * scale).reshape(bins, lags)
    return jnp.stack([cos, -sin]).astype(jnp.bfloat16)


def corr_kernel(src_ref, rec_ref, tab_ref, out_ref, rows_ref):
    n_win = src_ref.shape[1]
    n_src = src_ref.shape[2]
    n_cmp = src_ref.shape[4]
    n_rows = rec_ref.shape[2]
    for s in range(n_src):
        for i in range(n_cmp):
            acc_re = None
            acc_im = None
            for w in range(n_win):
                sre = src_ref[0, w, s, 0, pl.ds(i, 1), :]
                sim = src_ref[0, w, s, 1, pl.ds(i, 1), :]
                rre = rec_ref[w, 0]
                rim = rec_ref[w, 1]
                re = sre * rre + sim * rim
                im = sim * rre - sre * rim
                acc_re = re if acc_re is None else acc_re + re
                acc_im = im if acc_im is None else acc_im + im
            row = (s * n_cmp + i) * n_rows
            rows_ref[0, pl.ds(row, n_rows), :] = acc_re.astype(jnp.bfloat16)
            rows_ref[1, pl.ds(row, n_rows), :] = acc_im.astype(jnp.bfloat16)
    out_ref[0] = jnp.dot(rows_ref[0], tab_ref[0], preferred_element_type=jnp.float32) + jnp.dot(
        rows_ref[1], tab_ref[1], preferred_element_type=jnp.float32
    )


def correlate_all(picked_all, rec, table):
    steps, n_win, n_src, _, n_cmp, bins = picked_all.shape
    n_rows = rec.shape[2]
    lags = table.shape[2]
    m = n_src * n_cmp * n_rows
    return pl.pallas_call(
        corr_kernel,
        grid=(steps,),
        in_specs=[
            pl.BlockSpec((1, n_win, n_src, 2, n_cmp, bins), lambda t: (t, 0, 0, 0, 0, 0)),
            pl.BlockSpec(rec.shape, lambda t: (0, 0, 0, 0)),
            pl.BlockSpec(table.shape, lambda t: (0, 0, 0)),
        ],
        out_specs=pl.BlockSpec((1, m, lags), lambda t: (t, 0, 0)),
        out_shape=jax.ShapeDtypeStruct((steps, m, lags), jnp.float32),
        scratch_shapes=[pltpu.VMEM((2, m, bins), jnp.bfloat16)],
    )(picked_all, rec, table)


def on_device(spectra, flags, owners, source_slots):
    win_count = spectra.shape[0]
    bins = spectra.shape[4]
    weighted = whiten(spectra) * flags.astype(jnp.float32)[:, :, None, None, None]
    n_win = lax.axis_size(WIN)
    table = lag_table_fast(bins, NLAG, win_count * n_win)
    me = lax.axis_index(STA)
    chosen = []
    for step in range(STEPS):
        block = jnp.take(weighted, source_slots[step], axis=1)
        chosen.append(jnp.where(me == owners[step], block, 0.0))
    picked_all = jnp.stack(chosen)
    picked_all = broadcast_owner(picked_all)
    shape = weighted.shape
    rec = weighted.transpose(0, 2, 1, 3, 4).reshape(shape[0], 2, shape[1] * shape[3], shape[4])
    stacked = correlate_all(picked_all, rec, table).reshape(
        STEPS, shape[1], shape[3], shape[1], shape[3], NLAG
    )
    return sum_over(stacked, "c", "zl")


def solution(mesh):
    fine = fine_mesh(mesh)
    return jax.shard_map(
        on_device,
        mesh=fine,
        in_specs=(P(WIN, STA, None, None, None), P(WIN, STA), P(), P()),
        out_specs=P(None, None, None, STA, None, None),
        check_vma=False,
    )
```

profile of v0, /device:TPU:1, one launch (start us, length us, event | category | flops | bytes accessed | tf_op | source)
XLA Modules:
  0.0 213.7 jit_solution(1289157280942655089)
XLA Ops:
  0.0 1.5 fusion.18
  3.7 1.2 multiply_reduce_fusion
  6.0 1.1 divide_multiply_fusion
  7.2 0.9 gather_fusion
  8.1 0.9 gather_fusion.1
  10.2 0.9 gather_fusion.2
  11.1 0.9 gather_fusion.3
  13.9 1.6 all_to_all.39
  15.5 43.6 %all_to_all.47 = f32[32,1,9984]{2,1,0:T(1,128)S(1)} all-to-all(f32[32,1,9984]{2,1,0:T(1,128)S(1)} %all_to_all.39), channel_id=1, replica_groups=mesh['y'=8,'x'=4,'zh'=2,'zl'=4,'c'=2] {'y','x'}, dimensions={0} | all-to-all | bytes 2555904 | tf_op jit(solution)/shard_map/all_to_all | solution.py:30
  59.9 10.6 %collective-permute-start = (f32[9984]{0:T(1024)S(1)}, f32[9984]{0:T(1024)S(1)}, u32[]{:S(2)}, u32[]{:S(2)}) collective-permute-start(f32[9984]{0:T(1024)S(1)} %reduce_sum.46), channel_id=1, source_target_pairs={{0,8},{8,0},{1,9},{9,1},{2,10},{10,2},{3,11},{11,3},{4,12},{12,4},... | collective-permute-start | bytes 119816 | tf_op jit(solution)/shard_map/ppermute | solution.py:42
  70.5 1.4 collective-permute-done
  72.0 1.7 broadcast_in_dim.25
  73.7 4.9 %all-to-all-start.1 = ((f32[32,1,9984]{2,1,0:T(1,128)}), f32[32,1,9984]{2,1,0:T(1,128)}, u32[]{:S(2)}, u32[]{:S(2)}) async-start(f32[32,1,9984]{2,1,0:T(1,128)} %broadcast_in_dim.25), calls=%async_computation.1 | async-start | bytes 2555904 | tf_op jit(solution)/shard_map/all_to_all | solution.py:35
  78.9 3.4 %fusion.5 = (f32[1664,128]{0,1:T(8,128)S(1)}, f32[1664,128]{0,1:T(8,128)S(1)}) fusion(s32[1664]{0:T(1024)S(1)} %iota_add_fusion), kind=kLoop, calls=%fused_computation.15 | loop fusion | flops 1916928 | bytes 1710592 | tf_op jit(solution)/shard_map/cos | solution.py:75
  82.3 4.0 %multiply_convert_fusion = (bf16[1664,6,128]{0,2,1:T(8,128)(2,1)}, bf16[1664,6,128]{0,2,1:T(8,128)(2,1)}) fusion(f32[1664,128]{0,1:T(8,128)S(1)} %get-tuple-element.19, f32[1664,6]{0,1:T(8,128)S(1)} %get-tuple-element.17, f32[1664,128]{0,1:T(8,128)S(1)} %get-tuple-element.18, f32[1664,6]{0,1:T(8,128)S(1)} %get-tuple-element.16), kind=kLoop, calls=%fused_computation.6 | loop fusion | flops 14057472 | bytes 6895616 | tf_op jit(solution)/shard_map/convert.3
  86.3 4.6 %copy.27 = bf16[1,1664,768]{2,1,0:T(8,128)(2,1)S(1)} copy(bf16[1,1664,768]{1,2,0:T(8,128)(2,1)} %bitcast.49) | data formatting | bytes 5111808 | tf_op jit(solution)/shard_map/mul | solution.py:77
  90.8 4.5 %copy.28 = bf16[1,1664,768]{2,1,0:T(8,128)(2,1)} copy(bf16[1,1664,768]{1,2,0:T(8,128)(2,1)} %bitcast.48) | data formatting | bytes 5111808 | tf_op jit(solution)/shard_map/neg | solution.py:79
  96.2 4.4 %pad_maximum_fusion.tab_ref = bf16[2,1664,768]{2,1,0:T(8,128)(2,1)} fusion(bf16[1,1664,768]{2,1,0:T(8,128)(2,1)} %copy.28, bf16[1,1664,768]{2,1,0:T(8,128)(2,1)S(1)} %copy.27), kind=kLoop, calls=%fused_computation.4 | loop fusion | flops 2555904 | bytes 10223616 | tf_op jit(solution)/shard_map/stack | solution.py:79
  100.7 6.8 %all-to-all-done.1 = f32[32,1,9984]{2,1,0:T(1,128)} async-done(((f32[32,1,9984]{2,1,0:T(1,128)}), f32[32,1,9984]{2,1,0:T(1,128)}, u32[]{:S(2)}, u32[]{:S(2)}) %all-to-all-start.1) | async-done | bytes 1277984 | tf_op jit(solution)/shard_map/all_to_all | solution.py:35
  107.5 4.3 %reduce.5 = f32[32,9984]{1,0:T(8,128)S(1)} reduce(f32[32,1,9984]{2,1,0:T(1,128)} %all-to-all-done.1, f32[]{:T(128)} %constant.69), dimensions={1}, to_apply=%all_to_all.32.reduce_sub_computation | reduce | bytes 2555908 | tf_op jit(solution)/shard_map/all_to_all | solution.py:35
  111.8 1.7 reshape.284.src_ref
  113.5 8.6 %shard_map.46 = f32[4,144,768]{2,1,0:T(8,128)} custom-call(f32[4,2,4,2,3,1664]{5,4,3,2,1,0:T(4,128)} %reshape.284.src_ref, f32[2,2,12,1664]{3,2,1,0:T(8,128)} %copy.29.rec_ref, bf16[2,1664,768]{2,1,0:T(8,128)(2,1)} %pad_maximum_fusion.tab_ref), custom_call_target="tpu_custom_call" | custom-call | tf_op jit(solution)/shard_map/pallas_call | solution.py:113
  122.1 3.0 %all_to_all.40 = f32[2,1,221184]{2,1,0:T(1,128)S(1)} reshape(f32[4,144,768]{2,1,0:T(8,128)} %shard_map.46) | data formatting | bytes 3538944 | tf_op jit(solution)/shard_map/all_to_all | solution.py:30
  125.1 10.2 %all_to_all.48 = f32[2,1,221184]{2,1,0:T(1,128)S(1)} all-to-all(f32[2,1,221184]{2,1,0:T(1,128)S(1)} %all_to_all.40), channel_id=1, replica_groups=mesh['y'=8,'x'=4,'zh'=2,'zl'=4,'c'=2] {'c'}, dimensions={0} | all-to-all | bytes 3538944 | tf_op jit(solution)/shard_map/all_to_all | solution.py:30
  135.3 8.2 %reduce_sum.47 = f32[221184]{0:T(1024)S(1)} reduce(f32[2,1,221184]{2,1,0:T(1,128)S(1)} %all_to_all.48, f32[]{:T(128)} %constant.34.clone.1), dimensions={0,1}, to_apply=%region_3.5 | reduce | flops 221184 | bytes 2654212 | tf_op jit(solution)/shard_map/reduce_sum | solution.py:31
  143.6 25.5 %all_to_all.49 = f32[4,1,55296]{2,1,0:T(1,128)S(1)} all-to-all(f32[4,1,55296]{2,1,0:T(1,128)S(1)} %bitcast.50), channel_id=1, replica_groups=mesh['y'=8,'x'=4,'zh'=2,'zl'=4,'c'=2] {'zl'}, dimensions={0} | all-to-all | bytes 1769472 | tf_op jit(solution)/shard_map/all_to_all | solution.py:30
  170.4 24.4 %all_to_all.50 = f32[4,1,55296]{2,1,0:T(1,128)S(1)} all-to-all(f32[4,1,55296]{2,1,0:T(1,128)S(1)} %broadcast_in_dim.26), channel_id=1, replica_groups=mesh['y'=8,'x'=4,'zh'=2,'zl'=4,'c'=2] {'zl'}, dimensions={0} | all-to-all | bytes 1769472 | tf_op jit(solution)/shard_map/all_to_all | solution.py:35
  194.7 1.0 broadcast_in_dim.28
  195.7 6.5 %all_to_all.51 = f32[2,1,221184]{2,1,0:T(1,128)S(1)} all-to-all(f32[2,1,221184]{2,1,0:T(1,128)S(1)} %broadcast_in_dim.28), channel_id=1, replica_groups=mesh['y'=8,'x'=4,'zh'=2,'zl'=4,'c'=2] {'c'}, dimensions={0} | all-to-all | bytes 3538944 | tf_op jit(solution)/shard_map/all_to_all | solution.py:35
  202.2 6.4 %reduce.6 = f32[2,221184]{1,0:T(2,128)} reduce(f32[2,1,221184]{2,1,0:T(1,128)S(1)} %all_to_all.51, f32[]{:T(128)} %constant.69), dimensions={1}, to_apply=%all_to_all.38.reduce_sub_computation | reduce | bytes 3538948 | tf_op jit(solution)/shard_map/all_to_all | solution.py:35
  208.6 3.4 %reshape.286 = f32[4,4,3,4,3,768]{5,4,3,2,1,0:T(4,128)S(1)} reshape(f32[2,221184]{1,0:T(2,128)} %reduce.6) | data formatting | bytes 3538944 | tf_op jit(solution)/shard_map/reshape | solution.py:51
  212.0 1.7 copy.32
  (23 shorter events, 7.0 us)
Async XLA Ops:
  59.9 12.1 %collective-permute-start = (f32[9984]{0:T(1024)S(1)}, f32[9984]{0:T(1024)S(1)}, u32[]{:S(2)}, u32[]{:S(2)}) collective-permute-start(f32[9984]{0:T(1024)S(1)} %reduce_sum.46), channel_id=1, source_target_pairs={{0,8},{8,0},{1,9},{9,1},{2,10},{10,2},{3,11},{11,3},{4,12},{12,4},... | collective-permute-start | bytes 119816 | tf_op jit(solution)/shard_map/ppermute | solution.py:42
  73.7 33.8 %all-to-all-start.1 = ((f32[32,1,9984]{2,1,0:T(1,128)}), f32[32,1,9984]{2,1,0:T(1,128)}, u32[]{:S(2)}, u32[]{:S(2)}) async-start(f32[32,1,9984]{2,1,0:T(1,128)} %broadcast_in_dim.25), calls=%async_computation.1 | async-start | bytes 2555904 | tf_op jit(solution)/shard_map/all_to_all | solution.py:35
where the time goes:
time: 214 us
  blocking collectives  110 us (51%)
  other arithmetic  38.1 us (18%)
  local copies, waits for them, and re-layouts  30.2 us (14%)
  starting transfers between devices  15.5 us (7%)
  Pallas kernels  8.62 us (4%)
  waiting for transfers between devices  8.22 us (4%)
  between operations  2.76 us (1%)
    all_to_all x3, blocking collectives, a2a_sum(): parts = lax.all_to_all(x.reshape(n, -1), axes, 0, 0, tiled=True)  79.4 us
    all_to_all x2, blocking collectives, a2a_gather(): lax.all_to_all(jnp.broadcast_to(x[None], (n, x.shape[0])), axes, 0, 0, ti...  30.9 us
    all_to_all x2, other arithmetic, a2a_gather(): lax.all_to_all(jnp.broadcast_to(x[None], (n, x.shape[0])), axes, 0, 0, ti...  10.7 us
    ppermute x1, starting transfers between devices, broadcast_owner(): piece = piece + lax.ppermute(piece, 'zh', [(0, 1), (1, 0)])  10.6 us
    reduce_sum x3, other arithmetic, a2a_sum(): return jnp.sum(parts.reshape(n, -1), axis=0)  9.78 us
    pallas_call x1, Pallas kernels, correlate_all(): pl.pallas_call(corr_kernel, grid=(steps,), in_specs=[pl.BlockSpec((1, n_w...  8.62 us
    all_to_all x1, waiting for transfers between devices, a2a_gather(): lax.all_to_all(jnp.broadcast_to(x[None], (n, x.shape[0])), axes, 0, 0, ti...  6.8 us
    reshape x2, local copies, waits for them, and re-layouts, sum_over(): return a2a_gather(part, axis, n).reshape(x.shape)  5.06 us
  transfers between devices with their start and end apart: 2, of which 2 were waited for; matrix products, arithmetic and copies ran while one was open for 10% of the time, Pallas kernels for 0%

commit v1 on v0

--- a/solution.py
+++ b/solution.py
@@ -10,6 +10,7 @@
 
 NLAG = 768
 STEPS = 4
+MESH_ID = pl.DeviceIdType.MESH
 STA = ("y", "x", "zh")
 WIN = ("zl", "c")
 
@@ -41,20 +42,6 @@
     piece = a2a_sum(masked, plane, n)
     piece = piece + lax.ppermute(piece, "zh", [(0, 1), (1, 0)])
     return a2a_gather(piece, plane, n).reshape(masked.shape)
-
-
-def sum_over(x, axis, inner):
-    n = lax.axis_size(axis)
-    part = a2a_sum(x, axis, n)
-    if inner is not None:
-        part = sum_over_inner(part, inner)
-    return a2a_gather(part, axis, n).reshape(x.shape)
-
-
-def sum_over_inner(x, axis):
-    n = lax.axis_size(axis)
-    part = a2a_sum(x, axis, n)
-    return a2a_gather(part, axis, n).reshape(x.shape)
 
 
 def whiten(spectra):
@@ -124,6 +111,81 @@
     )(picked_all, rec, table)
 
 
+def win_sum_kernel(x_ref, out_ref, a1, a2, r1, r2, r3, send_sem, recv_sem):
+    rows = x_ref.shape[0]
+    h, q, e = rows // 2, rows // 4, rows // 8
+    coords = [lax.axis_index(a) for a in STA + WIN]
+    zl, c = coords[3], coords[4]
+    b1 = zl % 2
+    b2 = zl // 2
+    peer_c = tuple(coords[:4]) + (1 - c,)
+    peer_1 = tuple(coords[:3]) + (zl + 1 - 2 * b1, c)
+    peer_2 = tuple(coords[:3]) + (zl + 2 - 4 * b2, c)
+
+    barrier = pltpu.get_barrier_semaphore()
+    for peer in (peer_c, peer_1, peer_2):
+        pl.semaphore_signal(barrier, inc=1, device_id=peer, device_id_type=MESH_ID)
+    pl.semaphore_wait(barrier, 3)
+
+    def copy(src, dst, k, peer):
+        return pltpu.make_async_remote_copy(
+            src_ref=src, dst_ref=dst, send_sem=send_sem.at[k], recv_sem=recv_sem.at[k],
+            device_id=peer, device_id_type=MESH_ID)
+
+    mine1 = pl.multiple_of(c * h, 8)
+    other1 = pl.multiple_of((1 - c) * h, 8)
+    cp = copy(x_ref.at[pl.ds(other1, h)], r1, 0, peer_c)
+    cp.start()
+    cp.wait()
+    a1[...] = x_ref[pl.ds(mine1, h), :] + r1[...]
+
+    mine2 = pl.multiple_of(b1 * q, 8)
+    other2 = pl.multiple_of((1 - b1) * q, 8)
+    cp = copy(a1.at[pl.ds(other2, q)], r2, 1, peer_1)
+    cp.start()
+    cp.wait()
+    a2[...] = a1[pl.ds(mine2, q), :] + r2[...]
+
+    mine3 = pl.multiple_of(b2 * e, 8)
+    other3 = pl.multiple_of((1 - b2) * e, 8)
+    cp = copy(a2.at[pl.ds(other3, e)], r3, 2, peer_2)
+    cp.start()
+    cp.wait()
+    base_q = pl.multiple_of(mine1 + mine2, 8)
+    at_e = pl.multiple_of(base_q + mine3, 8)
+    out_ref[pl.ds(at_e, e), :] = a2[pl.ds(mine3, e), :] + r3[...]
+
+    cp = copy(out_ref.at[pl.ds(at_e, e)], out_ref.at[pl.ds(at_e, e)], 3, peer_2)
+    cp.start()
+    cp.wait()
+    cp = copy(out_ref.at[pl.ds(base_q, q)], out_ref.at[pl.ds(base_q, q)], 4, peer_1)
+    cp.start()
+    cp.wait()
+    cp = copy(out_ref.at[pl.ds(mine1, h)], out_ref.at[pl.ds(mine1, h)], 5, peer_c)
+    cp.start()
+    cp.wait()
+
+
+def win_sum(x):
+    rows, cols = x.shape
+    return pl.pallas_call(
+        win_sum_kernel,
+        out_shape=jax.ShapeDtypeStruct((rows, cols), jnp.float32),
+        in_specs=[pl.BlockSpec(memory_space=pltpu.VMEM)],
+        out_specs=pl.BlockSpec(memory_space=pltpu.VMEM),
+        scratch_shapes=[
+            pltpu.VMEM((rows // 2, cols), jnp.float32),
+            pltpu.VMEM((rows // 4, cols), jnp.float32),
+            pltpu.VMEM((rows // 2, cols), jnp.float32),
+            pltpu.VMEM((rows // 4, cols), jnp.float32),
+            pltpu.VMEM((rows // 8, cols), jnp.float32),
+            pltpu.SemaphoreType.DMA((6,)),
+            pltpu.SemaphoreType.DMA((6,)),
+        ],
+        compiler_params=pltpu.CompilerParams(collective_id=0, has_side_effects=True),
+    )(x)
+
+
 def on_device(spectra, flags, owners, source_slots):
     win_count = spectra.shape[0]
     bins = spectra.shape[4]
@@ -142,7 +204,7 @@
     stacked = correlate_all(picked_all, rec, table).reshape(
         STEPS, shape[1], shape[3], shape[1], shape[3], NLAG
     )
-    return sum_over(stacked, "c", "zl")
+    return win_sum(stacked.reshape(-1, NLAG)).reshape(stacked.shape)
 
 
 def solution(mesh):

time: 214 us -> 184 us (0.86)
  blocking collectives: 110 us -> 43.6 us
  Pallas kernels: 8.62 us -> 65.9 us
  other arithmetic: 38.1 us -> 22.6 us
  local copies, waits for them, and re-layouts: 30.2 us -> 25.1 us
    pallas_call x0 -> x1, Pallas kernels: none -> 57.2 us  [win_sum(): pl.pallas_call(win_sum_kernel, out_shape=jax.ShapeDtypeStruct((rows, cols...]
    all_to_all x3 -> x1, blocking collectives: 79.4 us -> 43.6 us  [a2a_sum(): parts = lax.all_to_all(x.reshape(n, -1), axes, 0, 0, tiled=True)]
    all_to_all x2 -> x0, blocking collectives: 30.9 us -> none  [a2a_gather(): lax.all_to_all(jnp.broadcast_to(x[None], (n, x.shape[0])), axes, 0, 0, ti...]
    reduce_sum x3 -> x1, other arithmetic: 9.78 us -> 0.74 us  [a2a_sum(): return jnp.sum(parts.reshape(n, -1), axis=0)]
    all_to_all x2 -> x1, other arithmetic: 10.7 us -> 4.34 us  [a2a_gather(): lax.all_to_all(jnp.broadcast_to(x[None], (n, x.shape[0])), axes, 0, 0, ti...]
    all_to_all x2 -> x1, local copies, waits for them, and re-layouts: 4.63 us -> 1.65 us  [a2a_sum(): parts = lax.all_to_all(x.reshape(n, -1), axes, 0, 0, tiled=True)]
  transfers between devices with their start and end apart: 2 -> 2, of which waited for: 2 -> 2; matrix products, arithmetic and copies ran while one was open for 10% -> 12% of each run, Pallas kernels for 0% -> 0%
where the time goes in v1:
time: 184 us
  Pallas kernels  65.9 us (36%)
  blocking collectives  43.6 us (24%)
  local copies, waits for them, and re-layouts  25.1 us (14%)
  other arithmetic  22.6 us (12%)
  starting transfers between devices  15.5 us (8%)
  waiting for transfers between devices  8.22 us (4%)
  between operations  2.74 us (1%)
    pallas_call x1, Pallas kernels, win_sum(): pl.pallas_call(win_sum_kernel, out_shape=jax.ShapeDtypeStruct((rows, cols...  57.2 us
    all_to_all x1, blocking collectives, a2a_sum(): parts = lax.all_to_all(x.reshape(n, -1), axes, 0, 0, tiled=True)  43.6 us
    ppermute x1, starting transfers between devices, broadcast_owner(): piece = piece + lax.ppermute(piece, 'zh', [(0, 1), (1, 0)])  10.6 us
    pallas_call x1, Pallas kernels, correlate_all(): pl.pallas_call(corr_kernel, grid=(steps,), in_specs=[pl.BlockSpec((1, n_w...  8.62 us
    all_to_all x1, waiting for transfers between devices, a2a_gather(): lax.all_to_all(jnp.broadcast_to(x[None], (n, x.shape[0])), axes, 0, 0, ti...  6.8 us
    all_to_all x1, starting transfers between devices, a2a_gather(): lax.all_to_all(jnp.broadcast_to(x[None], (n, x.shape[0])), axes, 0, 0, ti...  4.85 us
    mul x1, local copies, waits for them, and re-layouts, lag_table_fast(): cos = ((ca * cb - sa * sb) * scale).reshape(bins, lags)  4.58 us
    neg x1, local copies, waits for them, and re-layouts, lag_table_fast(): return jnp.stack([cos, -sin]).astype(jnp.bfloat16)  4.52 us
  transfers between devices with their start and end apart: 2, of which 2 were waited for; matrix products, arithmetic and copies ran while one was open for 12% of the time, Pallas kernels for 0%

profile of v1, /device:TPU:1, one launch (start us, length us, event | category | flops | bytes accessed | tf_op | source)
XLA Modules:
  0.0 183.6 jit_solution(7197226711574052223)
XLA Ops:
  0.0 1.5 fusion.18
  2.8 0.8 compare_and_fusion.3
  3.7 1.2 multiply_reduce_fusion
  5.3 0.7 convert_element_type.28
  6.0 1.1 divide_multiply_fusion
  7.2 0.9 gather_fusion
  8.1 0.9 gather_fusion.1
  10.2 0.9 gather_fusion.2
  11.1 0.9 gather_fusion.3
  12.0 0.4 fusion.9
  12.8 0.6 pad_maximum_fusion.1
  13.4 0.4 copy.12
  13.9 1.6 all_to_all.13
  15.5 43.6 %all_to_all.16 = f32[32,1,9984]{2,1,0:T(1,128)S(1)} all-to-all(f32[32,1,9984]{2,1,0:T(1,128)S(1)} %all_to_all.13), channel_id=1, replica_groups=mesh['y'=8,'x'=4,'zh'=2,'zl'=4,'c'=2] {'y','x'}, dimensions={0} | all-to-all | bytes 2555904 | tf_op jit(solution)/shard_map/all_to_all | solution.py:31
  59.2 0.7 reduce_sum.28
  59.9 10.6 %collective-permute-start = (f32[9984]{0:T(1024)S(1)}, f32[9984]{0:T(1024)S(1)}, u32[]{:S(2)}, u32[]{:S(2)}) collective-permute-start(f32[9984]{0:T(1024)S(1)} %reduce_sum.28), channel_id=1, source_target_pairs={{0,8},{8,0},{1,9},{9,1},{2,10},{10,2},{3,11},{11,3},{4,12},{12,4},... | collective-permute-start | bytes 119816 | tf_op jit(solution)/shard_map/ppermute | solution.py:43
  70.5 1.4 collective-permute-done
  72.0 1.7 broadcast_in_dim.19
  73.7 4.9 %all-to-all-start.1 = ((f32[32,1,9984]{2,1,0:T(1,128)}), f32[32,1,9984]{2,1,0:T(1,128)}, u32[]{:S(2)}, u32[]{:S(2)}) async-start(f32[32,1,9984]{2,1,0:T(1,128)} %broadcast_in_dim.19), calls=%async_computation.1 | async-start | bytes 2555904 | tf_op jit(solution)/shard_map/all_to_all | solution.py:36
  78.9 3.4 %fusion.5 = (f32[1664,128]{0,1:T(8,128)S(1)}, f32[1664,128]{0,1:T(8,128)S(1)}) fusion(s32[1664]{0:T(1024)S(1)} %iota_add_fusion), kind=kLoop, calls=%fused_computation.15 | loop fusion | flops 1916928 | bytes 1710592 | tf_op jit(solution)/shard_map/cos | solution.py:62
  82.3 4.0 %multiply_convert_fusion = (bf16[1664,6,128]{0,2,1:T(8,128)(2,1)}, bf16[1664,6,128]{0,2,1:T(8,128)(2,1)}) fusion(f32[1664,128]{0,1:T(8,128)S(1)} %get-tuple-element.19, f32[1664,6]{0,1:T(8,128)S(1)} %get-tuple-element.17, f32[1664,128]{0,1:T(8,128)S(1)} %get-tuple-element.18, f32[1664,6]{0,1:T(8,128)S(1)} %get-tuple-element.16), kind=kLoop, calls=%fused_computation.6 | loop fusion | flops 14057472 | bytes 6895616 | tf_op jit(solution)/shard_map/convert.3
  86.3 4.6 %copy.14 = bf16[1,1664,768]{2,1,0:T(8,128)(2,1)S(1)} copy(bf16[1,1664,768]{1,2,0:T(8,128)(2,1)} %bitcast.48) | data formatting | bytes 5111808 | tf_op jit(solution)/shard_map/mul | solution.py:64
  90.8 4.5 %copy.15 = bf16[1,1664,768]{2,1,0:T(8,128)(2,1)} copy(bf16[1,1664,768]{1,2,0:T(8,128)(2,1)} %bitcast.47) | data formatting | bytes 5111808 | tf_op jit(solution)/shard_map/neg | solution.py:66
  95.4 0.8 copy.16.rec_ref
  96.2 4.4 %pad_maximum_fusion.tab_ref = bf16[2,1664,768]{2,1,0:T(8,128)(2,1)} fusion(bf16[1,1664,768]{2,1,0:T(8,128)(2,1)} %copy.15, bf16[1,1664,768]{2,1,0:T(8,128)(2,1)S(1)} %copy.14), kind=kLoop, calls=%fused_computation.4 | loop fusion | flops 2555904 | bytes 10223616 | tf_op jit(solution)/shard_map/stack | solution.py:66
  100.7 6.8 %all-to-all-done.1 = f32[32,1,9984]{2,1,0:T(1,128)} async-done(((f32[32,1,9984]{2,1,0:T(1,128)}), f32[32,1,9984]{2,1,0:T(1,128)}, u32[]{:S(2)}, u32[]{:S(2)}) %all-to-all-start.1) | async-done | bytes 1277984 | tf_op jit(solution)/shard_map/all_to_all | solution.py:36
  107.5 4.3 %reduce.3 = f32[32,9984]{1,0:T(8,128)S(1)} reduce(f32[32,1,9984]{2,1,0:T(1,128)} %all-to-all-done.1, f32[]{:T(128)} %constant.69), dimensions={1}, to_apply=%all_to_all.12.reduce_sub_computation | reduce | bytes 2555908 | tf_op jit(solution)/shard_map/all_to_all | solution.py:36
  111.8 1.7 reshape.261.src_ref
  113.5 8.6 %shard_map.46 = f32[4,144,768]{2,1,0:T(8,128)} custom-call(f32[4,2,4,2,3,1664]{5,4,3,2,1,0:T(4,128)} %reshape.261.src_ref, f32[2,2,12,1664]{3,2,1,0:T(8,128)} %copy.16.rec_ref, bf16[2,1664,768]{2,1,0:T(8,128)(2,1)} %pad_maximum_fusion.tab_ref), custom_call_target="tpu_custom_call" | custom-call | tf_op jit(solution)/shard_map/pallas_call | solution.py:100
  122.1 57.2 %shard_map.47 = f32[576,768]{1,0:T(8,128)} custom-call(f32[576,768]{1,0:T(8,128)} %bitcast.49), custom_call_target="tpu_custom_call" | custom-call | tf_op jit(solution)/shard_map/pallas_call | solution.py:171
  179.3 2.6 %reshape.263 = f32[4,4,3,4,3,768]{5,4,3,2,1,0:T(4,128)S(1)} reshape(f32[576,768]{1,0:T(8,128)} %shard_map.47) | data formatting | bytes 3538944 | tf_op jit(solution)/shard_map/reshape | solution.py:207
  182.0 1.7 copy.17
  (14 shorter events, 1.2 us)
Async XLA Ops:
  59.9 12.1 %collective-permute-start = (f32[9984]{0:T(1024)S(1)}, f32[9984]{0:T(1024)S(1)}, u32[]{:S(2)}, u32[]{:S(2)}) collective-permute-start(f32[9984]{0:T(1024)S(1)} %reduce_sum.28), channel_id=1, source_target_pairs={{0,8},{8,0},{1,9},{9,1},{2,10},{10,2},{3,11},{11,3},{4,12},{12,4},... | collective-permute-start | bytes 119816 | tf_op jit(solution)/shard_map/ppermute | solution.py:43
  73.7 33.8 %all-to-all-start.1 = ((f32[32,1,9984]{2,1,0:T(1,128)}), f32[32,1,9984]{2,1,0:T(1,128)}, u32[]{:S(2)}, u32[]{:S(2)}) async-start(f32[32,1,9984]{2,1,0:T(1,128)} %broadcast_in_dim.19), calls=%async_computation.1 | async-start | bytes 2555904 | tf_op jit(solution)/shard_map/all_to_all | solution.py:36

commit v2 on v1

--- a/solution.py
+++ b/solution.py
@@ -25,23 +25,6 @@
     nc = len({d.core_on_chip for d in devs[0, :]})
     nzl = n_win // nc
     return Mesh(devs.reshape(ny, nx, nzh, nzl, nc), STA + WIN)
-
-
-def a2a_sum(x, axes, n):
-    parts = lax.all_to_all(x.reshape(n, -1), axes, 0, 0, tiled=True)
-    return jnp.sum(parts.reshape(n, -1), axis=0)
-
-
-def a2a_gather(x, axes, n):
-    return lax.all_to_all(jnp.broadcast_to(x[None], (n, x.shape[0])), axes, 0, 0, tiled=True)
-
-
-def broadcast_owner(masked):
-    plane = ("y", "x")
-    n = lax.axis_size(plane)
-    piece = a2a_sum(masked, plane, n)
-    piece = piece + lax.ppermute(piece, "zh", [(0, 1), (1, 0)])
-    return a2a_gather(piece, plane, n).reshape(masked.shape)
 
 
 def whiten(spectra):
@@ -186,6 +169,78 @@
     )(x)
 
 
+def bcast_kernel(m_ref, out_ref, rs_recv, piece, zh_recv, send_rs, recv_rs, send_ag, recv_ag, zsem):
+    n = m_ref.shape[0]
+    y, x, zh, zl, c = (lax.axis_index(a) for a in STA + WIN)
+    nx = lax.axis_size("x")
+    me = y * nx + x
+
+    def plane_peer(p):
+        return (p // nx, p % nx, zh, zl, c)
+
+    zpeer = (y, x, 1 - zh, zl, c)
+    barrier = pltpu.get_barrier_semaphore()
+    for d in range(1, n):
+        pl.semaphore_signal(barrier, inc=1, device_id=plane_peer((me + d) % n), device_id_type=MESH_ID)
+    pl.semaphore_signal(barrier, inc=1, device_id=zpeer, device_id_type=MESH_ID)
+    pl.semaphore_wait(barrier, n)
+
+    copies = []
+    for d in range(1, n):
+        dst = (me + d) % n
+        cp = pltpu.make_async_remote_copy(
+            src_ref=m_ref.at[dst], dst_ref=rs_recv.at[me], send_sem=send_rs.at[d],
+            recv_sem=recv_rs.at[d], device_id=plane_peer(dst), device_id_type=MESH_ID)
+        cp.start()
+        copies.append(cp)
+    for cp in copies:
+        cp.wait()
+    total = m_ref[me]
+    for d in range(1, n):
+        total = total + rs_recv[(me + n - d) % n]
+    piece[...] = total
+
+    cp = pltpu.make_async_remote_copy(
+        src_ref=piece, dst_ref=zh_recv, send_sem=zsem.at[0], recv_sem=zsem.at[1],
+        device_id=zpeer, device_id_type=MESH_ID)
+    cp.start()
+    cp.wait()
+    out_ref[me] = piece[...] + zh_recv[...]
+
+    copies = []
+    for d in range(1, n):
+        dst = (me + d) % n
+        cp = pltpu.make_async_remote_copy(
+            src_ref=out_ref.at[me], dst_ref=out_ref.at[me], send_sem=send_ag.at[d],
+            recv_sem=recv_ag.at[d], device_id=plane_peer(dst), device_id_type=MESH_ID)
+        cp.start()
+        copies.append(cp)
+    for cp in copies:
+        cp.wait()
+
+
+def bcast(masked):
+    n = masked.shape[0]
+    shape = masked.shape
+    return pl.pallas_call(
+        bcast_kernel,
+        out_shape=jax.ShapeDtypeStruct(shape, jnp.float32),
+        in_specs=[pl.BlockSpec(memory_space=pltpu.VMEM)],
+        out_specs=pl.BlockSpec(memory_space=pltpu.VMEM),
+        scratch_shapes=[
+            pltpu.VMEM(shape, jnp.float32),
+            pltpu.VMEM(shape[1:], jnp.float32),
+            pltpu.VMEM(shape[1:], jnp.float32),
+            pltpu.SemaphoreType.DMA((n,)),
+            pltpu.SemaphoreType.DMA((n,)),
+            pltpu.SemaphoreType.DMA((n,)),
+            pltpu.SemaphoreType.DMA((n,)),
+            pltpu.SemaphoreType.DMA((2,)),
+        ],
+        compiler_params=pltpu.CompilerParams(collective_id=1, has_side_effects=True),
+    )(masked)
+
+
 def on_device(spectra, flags, owners, source_slots):
     win_count = spectra.shape[0]
     bins = spectra.shape[4]
@@ -198,7 +253,8 @@
         block = jnp.take(weighted, source_slots[step], axis=1)
         chosen.append(jnp.where(me == owners[step], block, 0.0))
     picked_all = jnp.stack(chosen)
-    picked_all = broadcast_owner(picked_all)
+    plane = lax.axis_size(("y", "x"))
+    picked_all = bcast(picked_all.reshape(plane, -1, 128)).reshape(picked_all.shape)
     shape = weighted.shape
     rec = weighted.transpose(0, 2, 1, 3, 4).reshape(shape[0], 2, shape[1] * shape[3], shape[4])
     stacked = correlate_all(picked_all, rec, table).reshape(

time: 184 us -> 190 us (1.033); the launches traced: 184 us -> 188 us
  Pallas kernels: 65.9 us -> 143 us
  blocking collectives: 43.6 us -> 0 us
  starting transfers between devices: 15.5 us -> 0 us
  waiting for transfers between devices: 8.22 us -> 0 us
  other arithmetic: 22.6 us -> 17.6 us
    pallas_call x0 -> x1, Pallas kernels: none -> 78.5 us  [bcast(): pl.pallas_call(bcast_kernel, out_shape=jax.ShapeDtypeStruct(shape, jnp.fl...]
    all_to_all x1 -> x0, blocking collectives: 43.6 us -> none  [a2a_sum(): parts = lax.all_to_all(x.reshape(n, -1), axes, 0, 0, tiled=True)]
    ppermute x1 -> x0, starting transfers between devices: 10.6 us -> none  [broadcast_owner(): piece = piece + lax.ppermute(piece, 'zh', [(0, 1), (1, 0)])]
    all_to_all x1 -> x0, waiting for transfers between devices: 6.8 us -> none  [a2a_gather(): lax.all_to_all(jnp.broadcast_to(x[None], (n, x.shape[0])), axes, 0, 0, ti...]
    all_to_all x1 -> x0, starting transfers between devices: 4.85 us -> none  [a2a_gather(): lax.all_to_all(jnp.broadcast_to(x[None], (n, x.shape[0])), axes, 0, 0, ti...]
    all_to_all x1 -> x0, other arithmetic: 4.34 us -> none  [a2a_gather(): lax.all_to_all(jnp.broadcast_to(x[None], (n, x.shape[0])), axes, 0, 0, ti...]
    reshape x1 -> x2, local copies, waits for them, and re-layouts: 1.67 us -> 4.75 us  [the longest x1 3.01 us: on_device(): bcast(picked_all.reshape(plane, -1, 128)).reshape(picked_all.shape)]
  transfers between devices with their start and end apart: 2 -> 0, of which waited for: 2 -> 0; matrix products, arithmetic and copies ran while one was open for 12% -> 0% of each run, Pallas kernels for 0% -> 0%
where the time goes in v2:
time: 190 us; the launch traced here: 188 us
  Pallas kernels  143 us (75%)
  local copies, waits for them, and re-layouts  24.8 us (13%)
  other arithmetic  17.6 us (9%)
  between operations  2.7 us (1%)
    pallas_call x1, Pallas kernels, bcast(): pl.pallas_call(bcast_kernel, out_shape=jax.ShapeDtypeStruct(shape, jnp.fl...  78.5 us
    pallas_call x1, Pallas kernels, win_sum(): pl.pallas_call(win_sum_kernel, out_shape=jax.ShapeDtypeStruct((rows, cols...  55.6 us
    pallas_call x1, Pallas kernels, correlate_all(): pl.pallas_call(corr_kernel, grid=(steps,), in_specs=[pl.BlockSpec((1, n_w...  8.63 us
    neg x1, local copies, waits for them, and re-layouts, lag_table_fast(): return jnp.stack([cos, -sin]).astype(jnp.bfloat16)  4.58 us
    mul x1, local copies, waits for them, and re-layouts, lag_table_fast(): cos = ((ca * cb - sa * sb) * scale).reshape(bins, lags)  4.51 us
    another operation x1, other arithmetic, lag_table_fast(): return jnp.stack([cos, -sin]).astype(jnp.bfloat16)  4.45 us
    reshape x2, local copies, waits for them, and re-layouts, on_device(): return win_sum(stacked.reshape(-1, NLAG)).reshape(stacked.shape)  4.31 us
    another operation x1, other arithmetic  3.99 us

profile of v2, /device:TPU:1, one launch (start us, length us, event | category | flops | bytes accessed | tf_op | source)
XLA Modules:
  0.0 187.7 jit_solution(1444957286761321536)
XLA Ops:
  0.0 1.5 fusion.18
  2.7 0.8 compare_and_fusion.3
  3.6 1.2 multiply_reduce_fusion
  4.8 0.1 reduce_sum.14
  4.9 0.1 reduce_sum.18
  5.1 0.1 div.21
  5.2 0.1 div.22
  5.3 0.7 convert_element_type.28
  6.0 1.1 divide_multiply_fusion
  7.1 0.9 gather_fusion
  8.0 0.9 gather_fusion.1
  8.9 0.4 fusion.9
  10.6 0.9 gather_fusion.2
  11.5 0.9 gather_fusion.3
  12.4 0.4 fusion.7
  12.8 0.6 pad_maximum_fusion.1
  13.4 0.4 copy.8
  13.9 1.7 reshape.253.m_ref
  15.6 78.5 %shard_map.46 = f32[32,78,128]{2,1,0:T(8,128)} custom-call(f32[32,78,128]{2,1,0:T(8,128)} %reshape.253.m_ref), custom_call_target="tpu_custom_call" | custom-call | tf_op jit(solution)/shard_map/pallas_call | solution.py:225
  94.1 3.0 %reshape.254.src_ref = f32[4,2,4,2,3,1664]{5,4,3,2,1,0:T(4,128)} reshape(f32[32,78,128]{2,1,0:T(8,128)} %shard_map.46) | data formatting | bytes 2555904 | tf_op jit(solution)/shard_map/reshape | solution.py:257
  97.1 3.4 %fusion.5 = (f32[1664,128]{0,1:T(8,128)S(1)}, f32[1664,128]{0,1:T(8,128)S(1)}) fusion(s32[1664]{0:T(1024)S(1)} %iota_add_fusion), kind=kLoop, calls=%fused_computation.15 | loop fusion | flops 1916928 | bytes 1710592 | tf_op jit(solution)/shard_map/cos | solution.py:45
  100.5 0.3 fusion.16
  100.8 4.0 %multiply_convert_fusion = (bf16[1664,6,128]{0,2,1:T(8,128)(2,1)}, bf16[1664,6,128]{0,2,1:T(8,128)(2,1)}) fusion(f32[1664,128]{0,1:T(8,128)S(1)} %get-tuple-element.19, f32[1664,6]{0,1:T(8,128)S(1)} %get-tuple-element.17, f32[1664,128]{0,1:T(8,128)S(1)} %get-tuple-element.18, f32[1664,6]{0,1:T(8,128)S(1)} %get-tuple-element.16), kind=kLoop, calls=%fused_computation.6 | loop fusion | flops 14057472 | bytes 6895616 | tf_op jit(solution)/shard_map/convert.3
  104.8 4.6 %copy.10 = bf16[1,1664,768]{2,1,0:T(8,128)(2,1)S(1)} copy(bf16[1,1664,768]{1,2,0:T(8,128)(2,1)} %bitcast.48) | data formatting | bytes 5111808 | tf_op jit(solution)/shard_map/neg | solution.py:49
  109.4 4.5 %copy.9 = bf16[1,1664,768]{2,1,0:T(8,128)(2,1)} copy(bf16[1,1664,768]{1,2,0:T(8,128)(2,1)} %bitcast.47) | data formatting | bytes 5111808 | tf_op jit(solution)/shard_map/mul | solution.py:47
  113.9 4.5 %pad_maximum_fusion.tab_ref = bf16[2,1664,768]{2,1,0:T(8,128)(2,1)} fusion(bf16[1,1664,768]{2,1,0:T(8,128)(2,1)S(1)} %copy.10, bf16[1,1664,768]{2,1,0:T(8,128)(2,1)} %copy.9), kind=kLoop, calls=%fused_computation.4 | loop fusion | flops 2555904 | bytes 10223616 | tf_op jit(solution)/shard_map/stack | solution.py:49
  118.4 0.8 copy.11.rec_ref
  119.2 8.6 %shard_map.47 = f32[4,144,768]{2,1,0:T(8,128)} custom-call(f32[4,2,4,2,3,1664]{5,4,3,2,1,0:T(4,128)} %reshape.254.src_ref, f32[2,2,12,1664]{3,2,1,0:T(8,128)} %copy.11.rec_ref, bf16[2,1664,768]{2,1,0:T(8,128)(2,1)} %pad_maximum_fusion.tab_ref), custom_call_target="tpu_custom_call" | custom-call | tf_op jit(solution)/shard_map/pallas_call | solution.py:83
  127.8 55.6 %shard_map.48 = f32[576,768]{1,0:T(8,128)} custom-call(f32[576,768]{1,0:T(8,128)} %bitcast.49), custom_call_target="tpu_custom_call" | custom-call | tf_op jit(solution)/shard_map/pallas_call | solution.py:154
  183.4 2.6 %reshape.256 = f32[4,4,3,4,3,768]{5,4,3,2,1,0:T(4,128)S(1)} reshape(f32[576,768]{1,0:T(8,128)} %shard_map.48) | data formatting | bytes 3538944 | tf_op jit(solution)/shard_map/reshape | solution.py:263
  186.1 1.7 copy.12
  (7 shorter events, 0.0 us)

commit v3 on v2

--- a/solution.py
+++ b/solution.py
@@ -1,3 +1,4 @@
+import functools
 import math
 
 import jax
@@ -34,26 +35,33 @@
     return (blocks / jnp.sqrt(power + 1e-06)).reshape(shape)
 
 
-def lag_table_fast(bins, lags, windows):
+def lag_factors(bins, lags):
     freq = jnp.arange(bins, dtype=jnp.int32) + 360
     q = jnp.arange(lags // 128, dtype=jnp.int32) * 128 - lags // 2
     k = jnp.arange(128, dtype=jnp.int32)
     unit = 2.0 * math.pi / 7200.0
     a = jnp.mod(freq[:, None] * q[None, :], 7200).astype(jnp.float32) * unit
     b = jnp.mod(freq[:, None] * k[None, :], 7200).astype(jnp.float32) * unit
-    ca, sa = jnp.cos(a)[:, :, None], jnp.sin(a)[:, :, None]
-    cb, sb = jnp.cos(b)[:, None, :], jnp.sin(b)[:, None, :]
-    scale = 1.0 / math.sqrt(windows * bins)
-    cos = ((ca * cb - sa * sb) * scale).reshape(bins, lags)
-    sin = ((sa * cb + ca * sb) * scale).reshape(bins, lags)
-    return jnp.stack([cos, -sin]).astype(jnp.bfloat16)
-
-
-def corr_kernel(src_ref, rec_ref, tab_ref, out_ref, rows_ref):
+    return jnp.cos(a), jnp.sin(a), jnp.cos(b), jnp.sin(b)
+
+
+def corr_kernel(scale, src_ref, rec_ref, ca_ref, sa_ref, cb_ref, sb_ref, out_ref, rows_ref, tab_ref):
     n_win = src_ref.shape[1]
     n_src = src_ref.shape[2]
     n_cmp = src_ref.shape[4]
     n_rows = rec_ref.shape[2]
+
+    @pl.when(pl.program_id(0) == 0)
+    def _():
+        cb = cb_ref[...]
+        sb = sb_ref[...]
+        for q in range(ca_ref.shape[1]):
+            ca = ca_ref[:, pl.ds(q, 1)]
+            sa = sa_ref[:, pl.ds(q, 1)]
+            cols = pl.ds(q * 128, 128)
+            tab_ref[0, :, cols] = ((ca * cb - sa * sb) * scale).astype(jnp.bfloat16)
+            tab_ref[1, :, cols] = (-((sa * cb + ca * sb) * scale)).astype(jnp.bfloat16)
+
     for s in range(n_src):
         for i in range(n_cmp):
             acc_re = None
@@ -75,23 +83,28 @@
     )
 
 
-def correlate_all(picked_all, rec, table):
+def correlate_all(picked_all, rec, factors, windows):
     steps, n_win, n_src, _, n_cmp, bins = picked_all.shape
     n_rows = rec.shape[2]
-    lags = table.shape[2]
+    lags = NLAG
     m = n_src * n_cmp * n_rows
+    scale = 1.0 / math.sqrt(windows * bins)
+    whole = lambda t: (0, 0)
     return pl.pallas_call(
-        corr_kernel,
+        functools.partial(corr_kernel, scale),
         grid=(steps,),
         in_specs=[
             pl.BlockSpec((1, n_win, n_src, 2, n_cmp, bins), lambda t: (t, 0, 0, 0, 0, 0)),
             pl.BlockSpec(rec.shape, lambda t: (0, 0, 0, 0)),
-            pl.BlockSpec(table.shape, lambda t: (0, 0, 0)),
-        ],
+        ]
+        + [pl.BlockSpec(f.shape, whole) for f in factors],
         out_specs=pl.BlockSpec((1, m, lags), lambda t: (t, 0, 0)),
         out_shape=jax.ShapeDtypeStruct((steps, m, lags), jnp.float32),
-        scratch_shapes=[pltpu.VMEM((2, m, bins), jnp.bfloat16)],
-    )(picked_all, rec, table)
+        scratch_shapes=[
+            pltpu.VMEM((2, m, bins), jnp.bfloat16),
+            pltpu.VMEM((2, bins, lags), jnp.bfloat16),
+        ],
+    )(picked_all, rec, *factors)
 
 
 def win_sum_kernel(x_ref, out_ref, a1, a2, r1, r2, r3, send_sem, recv_sem):
@@ -246,7 +259,7 @@
     bins = spectra.shape[4]
     weighted = whiten(spectra) * flags.astype(jnp.float32)[:, :, None, None, None]
     n_win = lax.axis_size(WIN)
-    table = lag_table_fast(bins, NLAG, win_count * n_win)
+    factors = lag_factors(bins, NLAG)
     me = lax.axis_index(STA)
     chosen = []
     for step in range(STEPS):
@@ -257,7 +270,7 @@
     picked_all = bcast(picked_all.reshape(plane, -1, 128)).reshape(picked_all.shape)
     shape = weighted.shape
     rec = weighted.transpose(0, 2, 1, 3, 4).reshape(shape[0], 2, shape[1] * shape[3], shape[4])
-    stacked = correlate_all(picked_all, rec, table).reshape(
+    stacked = correlate_all(picked_all, rec, factors, win_count * n_win).reshape(
         STEPS, shape[1], shape[3], shape[1], shape[3], NLAG
     )
     return win_sum(stacked.reshape(-1, NLAG)).reshape(stacked.shape)

time: 190 us -> 180 us (0.947)
  local copies, waits for them, and re-layouts: 24.8 us -> 16 us
  other arithmetic: 17.6 us -> 13.8 us
  Pallas kernels: 143 us -> 146 us
    sin x0 -> x2, other arithmetic: none -> 9.19 us  [lag_factors(): return (jnp.cos(a), jnp.sin(a), jnp.cos(b), jnp.sin(b))]
    another operation x2 -> x0, other arithmetic: 8.44 us -> none  [the longest x1 4.45 us: lag_table_fast(): return jnp.stack([cos, -sin]).astype(jnp.bfloat16)]
    neg x1 -> x0, local copies, waits for them, and re-layouts: 4.58 us -> none  [lag_table_fast(): return jnp.stack([cos, -sin]).astype(jnp.bfloat16)]
    mul x1 -> x0, local copies, waits for them, and re-layouts: 4.51 us -> none  [lag_table_fast(): cos = ((ca * cb - sa * sb) * scale).reshape(bins, lags)]
    cos x2 -> x0, other arithmetic: 3.72 us -> none  [the longest x1 3.42 us: lag_table_fast(): cb, sb = (jnp.cos(b)[:, None, :], jnp.sin(b)[:, None, :])]
    pallas_call x1, Pallas kernels: 8.63 us -> 11.5 us  [correlate_all(): pl.pallas_call(functools.partial(corr_kernel, scale), grid=(steps,), in_s...]
where the time goes in v3:
time: 180 us; the launch traced here: 178 us
  Pallas kernels  146 us (81%)
  local copies, waits for them, and re-layouts  16 us (9%)
  other arithmetic  13.8 us (8%)
  between operations  2.71 us (2%)
    pallas_call x1, Pallas kernels, bcast(): pl.pallas_call(bcast_kernel, out_shape=jax.ShapeDtypeStruct(shape, jnp.fl...  78.5 us
    pallas_call x1, Pallas kernels, win_sum(): pl.pallas_call(win_sum_kernel, out_shape=jax.ShapeDtypeStruct((rows, cols...  55.6 us
    pallas_call x1, Pallas kernels, correlate_all(): pl.pallas_call(functools.partial(corr_kernel, scale), grid=(steps,), in_s...  11.5 us
    sin x2, other arithmetic, lag_factors(): return (jnp.cos(a), jnp.sin(a), jnp.cos(b), jnp.sin(b))  9.19 us
    reshape x2, local copies, waits for them, and re-layouts, on_device(): return win_sum(stacked.reshape(-1, NLAG)).reshape(stacked.shape)  4.31 us
    gather x4, local copies, waits for them, and re-layouts, on_device(): block = jnp.take(weighted, source_slots[step], axis=1)  3.61 us

profile of v3, /device:TPU:1, one launch (start us, length us, event | category | flops | bytes accessed | tf_op | source)
XLA Modules:
  0.0 178.0 jit_solution(8428291154267784801)
XLA Ops:
  0.0 0.0 copy-start
  0.0 0.7 convert_element_type.13
  0.7 1.5 fusion.15
  4.7 0.8 compare_and_fusion.3
  5.6 0.1 fusion.11
  5.7 1.2 multiply_reduce_fusion
  6.9 0.1 reduce_sum.14
  7.1 0.1 reduce_sum.18
  7.2 0.1 div.21
  7.3 0.1 div.22
  7.4 0.0 copy-done
  7.4 0.2 divide_multiply_fusion
  7.6 0.9 gather_fusion.3
  8.5 0.9 gather_fusion.2
  9.4 0.4 fusion.7
  9.8 0.9 gather_fusion.1
  10.7 0.9 gather_fusion
  11.6 0.4 fusion.9
  12.0 0.6 pad_maximum_fusion
  12.6 0.4 copy.11
  13.1 1.7 reshape.39.m_ref
  14.8 78.5 %shard_map.46 = f32[32,78,128]{2,1,0:T(8,128)} custom-call(f32[32,78,128]{2,1,0:T(8,128)} %reshape.39.m_ref), custom_call_target="tpu_custom_call" | custom-call | tf_op jit(solution)/shard_map/pallas_call | solution.py:238
  93.3 3.0 %reshape.40.src_ref = f32[4,2,4,2,3,1664]{5,4,3,2,1,0:T(4,128)} reshape(f32[32,78,128]{2,1,0:T(8,128)} %shard_map.46) | data formatting | bytes 2555904 | tf_op jit(solution)/shard_map/reshape | solution.py:270
  96.3 0.8 copy.13.rec_ref
  97.1 0.3 copy.12
  97.4 3.8 %multiply_sine_fusion = (f32[1664,6]{1,0:T(8,128)}, f32[1664,6]{1,0:T(8,128)}) fusion(f32[1664,6]{1,0:T(8,128)S(1)} %copy.12), kind=kLoop, calls=%fused_computation.14 | loop fusion | flops 9984 | bytes 119808 | tf_op jit(solution)/shard_map/sin | solution.py:45
  101.2 5.4 %fusion.4 = (f32[1664,128]{1,0:T(8,128)}, f32[1664,128]{1,0:T(8,128)}) fusion(s32[1664]{0:T(1024)S(1)} %iota_add_fusion), kind=kLoop, calls=%fused_computation.11 | loop fusion | flops 1916928 | bytes 1710592 | tf_op jit(solution)/shard_map/sin | solution.py:45
  106.6 11.5 %shard_map.47 = f32[4,144,768]{2,1,0:T(8,128)} custom-call(f32[4,2,4,2,3,1664]{5,4,3,2,1,0:T(4,128)} %reshape.40.src_ref, f32[2,2,12,1664]{3,2,1,0:T(8,128)} %copy.13.rec_ref, f32[1664,6]{1,0:T(8,128)} %get-tuple-element.15.ca_ref, f32[1664,6]{1,0:T(8,128)} %get-tuple-element.14.sa_ref, f32[1664,128]{1,0:T(8,128)} %get-tuple-element.17.cb_ref, ...), custom_call_target="tpu_custom_call" | custom-call | tf_op jit(solution)/shard_map/pallas_call | solution.py:93
  118.1 55.6 %shard_map.48 = f32[576,768]{1,0:T(8,128)} custom-call(f32[576,768]{1,0:T(8,128)} %bitcast.45), custom_call_target="tpu_custom_call" | custom-call | tf_op jit(solution)/shard_map/pallas_call | solution.py:167
  173.7 2.6 %reshape.42 = f32[4,4,3,4,3,768]{5,4,3,2,1,0:T(4,128)S(1)} reshape(f32[576,768]{1,0:T(8,128)} %shard_map.48) | data formatting | bytes 3538944 | tf_op jit(solution)/shard_map/reshape | solution.py:276
  176.4 1.7 copy.14
  (7 shorter events, 0.0 us)
Async XLA Ops:
  0.0 7.4 %copy-start = (f32[2,4,2,3,1664]{4,2,3,1,0:T(2,128)S(1)}, f32[2,4,2,3,1664]{4,2,3,1,0:T(2,128)}, u32[]{:S(2)}) copy-start(f32[2,4,2,3,1664]{4,2,3,1,0:T(2,128)} %param.6) | copy-start | bytes 958468

commit v4 on v3

--- a/solution.py
+++ b/solution.py
@@ -35,17 +35,17 @@
     return (blocks / jnp.sqrt(power + 1e-06)).reshape(shape)
 
 
-def lag_factors(bins, lags):
+def lag_phases(bins, lags):
     freq = jnp.arange(bins, dtype=jnp.int32) + 360
     q = jnp.arange(lags // 128, dtype=jnp.int32) * 128 - lags // 2
     k = jnp.arange(128, dtype=jnp.int32)
     unit = 2.0 * math.pi / 7200.0
     a = jnp.mod(freq[:, None] * q[None, :], 7200).astype(jnp.float32) * unit
     b = jnp.mod(freq[:, None] * k[None, :], 7200).astype(jnp.float32) * unit
-    return jnp.cos(a), jnp.sin(a), jnp.cos(b), jnp.sin(b)
-
-
-def corr_kernel(scale, src_ref, rec_ref, ca_ref, sa_ref, cb_ref, sb_ref, out_ref, rows_ref, tab_ref):
+    return a, b
+
+
+def corr_kernel(scale, src_ref, rec_ref, a_ref, b_ref, out_ref, rows_ref, tab_ref):
     n_win = src_ref.shape[1]
     n_src = src_ref.shape[2]
     n_cmp = src_ref.shape[4]
@@ -53,11 +53,13 @@
 
     @pl.when(pl.program_id(0) == 0)
     def _():
-        cb = cb_ref[...]
-        sb = sb_ref[...]
-        for q in range(ca_ref.shape[1]):
-            ca = ca_ref[:, pl.ds(q, 1)]
-            sa = sa_ref[:, pl.ds(q, 1)]
+        b = b_ref[...]
+        cb = jnp.cos(b)
+        sb = jnp.sin(b)
+        for q in range(a_ref.shape[1]):
+            a = a_ref[:, pl.ds(q, 1)]
+            ca = jnp.cos(a)
+            sa = jnp.sin(a)
             cols = pl.ds(q * 128, 128)
             tab_ref[0, :, cols] = ((ca * cb - sa * sb) * scale).astype(jnp.bfloat16)
             tab_ref[1, :, cols] = (-((sa * cb + ca * sb) * scale)).astype(jnp.bfloat16)
@@ -259,7 +261,7 @@
     bins = spectra.shape[4]
     weighted = whiten(spectra) * flags.astype(jnp.float32)[:, :, None, None, None]
     n_win = lax.axis_size(WIN)
-    factors = lag_factors(bins, NLAG)
+    factors = lag_phases(bins, NLAG)
     me = lax.axis_index(STA)
     chosen = []
     for step in range(STEPS):

time: 180 us -> 192 us (1.067)
  Pallas kernels: 146 us -> 165 us
  other arithmetic: 13.8 us -> 7.68 us
    pallas_call x1, Pallas kernels: 11.5 us -> 30.6 us  [correlate_all(): pl.pallas_call(functools.partial(corr_kernel, scale), grid=(steps,), in_s...]
    sin x2 -> x0, other arithmetic: 9.19 us -> none  [lag_factors(): return (jnp.cos(a), jnp.sin(a), jnp.cos(b), jnp.sin(b))]
    mul x0 -> x2, other arithmetic: none -> 3.21 us  [the longest x1 1.62 us: lag_phases(): b = jnp.mod(freq[:, None] * k[None, :], 7200).astype(jnp.float32) * unit]
where the time goes in v4:
time: 192 us; the launch traced here: 191 us
  Pallas kernels  165 us (86%)
  local copies, waits for them, and re-layouts  15.5 us (8%)
  other arithmetic  7.68 us (4%)
  between operations  2.71 us (1%)
    pallas_call x1, Pallas kernels, bcast(): pl.pallas_call(bcast_kernel, out_shape=jax.ShapeDtypeStruct(shape, jnp.fl...  78.4 us
    pallas_call x1, Pallas kernels, win_sum(): pl.pallas_call(win_sum_kernel, out_shape=jax.ShapeDtypeStruct((rows, cols...  55.6 us
    pallas_call x1, Pallas kernels, correlate_all(): pl.pallas_call(functools.partial(corr_kernel, scale), grid=(steps,), in_s...  30.6 us
    reshape x2, local copies, waits for them, and re-layouts, on_device(): return win_sum(stacked.reshape(-1, NLAG)).reshape(stacked.shape)  4.31 us

profile of v4, /device:TPU:1, one launch (start us, length us, event | category | flops | bytes accessed | tf_op | source)
XLA Modules:
  0.0 190.5 jit_solution(10819196181311823483)
XLA Ops:
  0.0 0.0 copy-start
  0.0 0.7 convert_element_type.9
  0.7 1.5 fusion.14
  4.7 0.8 compare_and_fusion.3
  5.7 1.2 multiply_reduce_fusion
  6.9 0.1 reduce_sum.14
  7.0 0.1 reduce_sum.18
  7.1 0.1 div.21
  7.2 0.1 div.22
  7.3 0.0 copy-done
  7.3 0.2 divide_multiply_fusion
  7.5 0.9 gather_fusion.3
  8.4 0.9 gather_fusion.2
  9.3 0.4 fusion.10
  9.7 0.9 gather_fusion.1
  10.6 0.9 gather_fusion
  11.6 0.4 fusion.12
  12.0 0.6 pad_maximum_fusion
  12.5 0.4 copy.11
  13.0 1.6 reshape.39.m_ref
  14.5 78.4 %shard_map.46 = f32[32,78,128]{2,1,0:T(8,128)} custom-call(f32[32,78,128]{2,1,0:T(8,128)} %reshape.39.m_ref), custom_call_target="tpu_custom_call" | custom-call | tf_op jit(solution)/shard_map/pallas_call | solution.py:240
  93.0 3.0 %reshape.40.src_ref = f32[4,2,4,2,3,1664]{5,4,3,2,1,0:T(4,128)} reshape(f32[32,78,128]{2,1,0:T(8,128)} %shard_map.46) | data formatting | bytes 2555904 | tf_op jit(solution)/shard_map/reshape | solution.py:272
  96.0 0.8 copy.13.rec_ref
  96.8 1.6 fusion.1.a_ref
  98.4 1.6 fusion.3.b_ref
  100.0 30.6 %shard_map.47 = f32[4,144,768]{2,1,0:T(8,128)} custom-call(f32[4,2,4,2,3,1664]{5,4,3,2,1,0:T(4,128)} %reshape.40.src_ref, f32[2,2,12,1664]{3,2,1,0:T(8,128)} %copy.13.rec_ref, f32[1664,6]{1,0:T(8,128)} %fusion.1.a_ref, f32[1664,128]{1,0:T(8,128)} %fusion.3.b_ref), custom_call_target="tpu_custom_call" | custom-call | tf_op jit(solution)/shard_map/pallas_call | solution.py:95
  130.6 55.6 %shard_map.48 = f32[576,768]{1,0:T(8,128)} custom-call(f32[576,768]{1,0:T(8,128)} %bitcast.45), custom_call_target="tpu_custom_call" | custom-call | tf_op jit(solution)/shard_map/pallas_call | solution.py:169
  186.2 2.6 %reshape.42 = f32[4,4,3,4,3,768]{5,4,3,2,1,0:T(4,128)S(1)} reshape(f32[576,768]{1,0:T(8,128)} %shard_map.48) | data formatting | bytes 3538944 | tf_op jit(solution)/shard_map/reshape | solution.py:278
  188.8 1.7 copy.14
  (7 shorter events, 0.0 us)
Async XLA Ops:
  0.0 7.3 %copy-start = (f32[2,4,2,3,1664]{4,2,3,1,0:T(2,128)S(1)}, f32[2,4,2,3,1664]{4,2,3,1,0:T(2,128)}, u32[]{:S(2)}) copy-start(f32[2,4,2,3,1664]{4,2,3,1,0:T(2,128)} %param.6) | copy-start | bytes 958468

commit v5 on v3

--- a/solution.py
+++ b/solution.py
@@ -182,59 +182,59 @@
     )(x)
 
 
-def bcast_kernel(m_ref, out_ref, rs_recv, piece, zh_recv, send_rs, recv_rs, send_ag, recv_ag, zsem):
-    n = m_ref.shape[0]
+def bcast_kernel(m_ref, out_ref, rx, s1, ry, piece, zr, sx, rxs, sy, rys, agy_s, agy_r, agx_s, agx_r, zsem):
+    nx, ny = m_ref.shape[0], m_ref.shape[1]
     y, x, zh, zl, c = (lax.axis_index(a) for a in STA + WIN)
-    nx = lax.axis_size("x")
-    me = y * nx + x
-
-    def plane_peer(p):
-        return (p // nx, p % nx, zh, zl, c)
-
+    xpeer = lambda p: (y, p, zh, zl, c)
+    ypeer = lambda p: (p, x, zh, zl, c)
     zpeer = (y, x, 1 - zh, zl, c)
+
     barrier = pltpu.get_barrier_semaphore()
-    for d in range(1, n):
-        pl.semaphore_signal(barrier, inc=1, device_id=plane_peer((me + d) % n), device_id_type=MESH_ID)
+    for d in range(1, nx):
+        pl.semaphore_signal(barrier, inc=1, device_id=xpeer((x + d) % nx), device_id_type=MESH_ID)
+    for d in range(1, ny):
+        pl.semaphore_signal(barrier, inc=1, device_id=ypeer((y + d) % ny), device_id_type=MESH_ID)
     pl.semaphore_signal(barrier, inc=1, device_id=zpeer, device_id_type=MESH_ID)
-    pl.semaphore_wait(barrier, n)
-
-    copies = []
-    for d in range(1, n):
-        dst = (me + d) % n
-        cp = pltpu.make_async_remote_copy(
-            src_ref=m_ref.at[dst], dst_ref=rs_recv.at[me], send_sem=send_rs.at[d],
-            recv_sem=recv_rs.at[d], device_id=plane_peer(dst), device_id_type=MESH_ID)
-        cp.start()
-        copies.append(cp)
-    for cp in copies:
-        cp.wait()
-    total = m_ref[me]
-    for d in range(1, n):
-        total = total + rs_recv[(me + n - d) % n]
-    piece[...] = total
+    pl.semaphore_wait(barrier, nx + ny - 1)
+
+    def send_all(n, me, peer, src, dst, ssem, rsem):
+        copies = []
+        for d in range(1, n):
+            to = (me + d) % n
+            cp = pltpu.make_async_remote_copy(
+                src_ref=src(to), dst_ref=dst, send_sem=ssem.at[d], recv_sem=rsem.at[d],
+                device_id=peer(to), device_id_type=MESH_ID)
+            cp.start()
+            copies.append(cp)
+        for cp in copies:
+            cp.wait()
+
+    send_all(nx, x, xpeer, lambda to: m_ref.at[to], rx.at[x], sx, rxs)
+    total = m_ref[x]
+    for d in range(1, nx):
+        total = total + rx[(x + nx - d) % nx]
+    s1[...] = total
+
+    send_all(ny, y, ypeer, lambda to: s1.at[to], ry.at[y], sy, rys)
+    part = s1[y]
+    for d in range(1, ny):
+        part = part + ry[(y + ny - d) % ny]
+    piece[...] = part
 
     cp = pltpu.make_async_remote_copy(
-        src_ref=piece, dst_ref=zh_recv, send_sem=zsem.at[0], recv_sem=zsem.at[1],
+        src_ref=piece, dst_ref=zr, send_sem=zsem.at[0], recv_sem=zsem.at[1],
         device_id=zpeer, device_id_type=MESH_ID)
     cp.start()
     cp.wait()
-    out_ref[me] = piece[...] + zh_recv[...]
-
-    copies = []
-    for d in range(1, n):
-        dst = (me + d) % n
-        cp = pltpu.make_async_remote_copy(
-            src_ref=out_ref.at[me], dst_ref=out_ref.at[me], send_sem=send_ag.at[d],
-            recv_sem=recv_ag.at[d], device_id=plane_peer(dst), device_id_type=MESH_ID)
-        cp.start()
-        copies.append(cp)
-    for cp in copies:
-        cp.wait()
+    out_ref[x, y] = piece[...] + zr[...]
+
+    send_all(ny, y, ypeer, lambda to: out_ref.at[x, y], out_ref.at[x, y], agy_s, agy_r)
+    send_all(nx, x, xpeer, lambda to: out_ref.at[x], out_ref.at[x], agx_s, agx_r)
 
 
 def bcast(masked):
-    n = masked.shape[0]
     shape = masked.shape
+    nx, ny = shape[0], shape[1]
     return pl.pallas_call(
         bcast_kernel,
         out_shape=jax.ShapeDtypeStruct(shape, jnp.float32),
@@ -244,10 +244,16 @@
             pltpu.VMEM(shape, jnp.float32),
             pltpu.VMEM(shape[1:], jnp.float32),
             pltpu.VMEM(shape[1:], jnp.float32),
-            pltpu.SemaphoreType.DMA((n,)),
-            pltpu.SemaphoreType.DMA((n,)),
-            pltpu.SemaphoreType.DMA((n,)),
-            pltpu.SemaphoreType.DMA((n,)),
+            pltpu.VMEM(shape[2:], jnp.float32),
+            pltpu.VMEM(shape[2:], jnp.float32),
+            pltpu.SemaphoreType.DMA((nx,)),
+            pltpu.SemaphoreType.DMA((nx,)),
+            pltpu.SemaphoreType.DMA((ny,)),
+            pltpu.SemaphoreType.DMA((ny,)),
+            pltpu.SemaphoreType.DMA((ny,)),
+            pltpu.SemaphoreType.DMA((ny,)),
+            pltpu.SemaphoreType.DMA((nx,)),
+            pltpu.SemaphoreType.DMA((nx,)),
             pltpu.SemaphoreType.DMA((2,)),
         ],
         compiler_params=pltpu.CompilerParams(collective_id=1, has_side_effects=True),
@@ -266,8 +272,8 @@
         block = jnp.take(weighted, source_slots[step], axis=1)
         chosen.append(jnp.where(me == owners[step], block, 0.0))
     picked_all = jnp.stack(chosen)
-    plane = lax.axis_size(("y", "x"))
-    picked_all = bcast(picked_all.reshape(plane, -1, 128)).reshape(picked_all.shape)
+    split = (lax.axis_size("x"), lax.axis_size("y"), -1, 128)
+    picked_all = bcast(picked_all.reshape(split)).reshape(picked_all.shape)
     shape = weighted.shape
     rec = weighted.transpose(0, 2, 1, 3, 4).reshape(shape[0], 2, shape[1] * shape[3], shape[4])
     stacked = correlate_all(picked_all, rec, factors, win_count * n_win).reshape(

time: 180 us -> 166 us (0.922)
  Pallas kernels: 146 us -> 132 us
    pallas_call x1, Pallas kernels: 78.5 us -> 63.3 us  [bcast(): pl.pallas_call(bcast_kernel, out_shape=jax.ShapeDtypeStruct(shape, jnp.fl...]
    pallas_call x1, Pallas kernels: 55.6 us -> 57.5 us  [win_sum(): pl.pallas_call(win_sum_kernel, out_shape=jax.ShapeDtypeStruct((rows, cols...]
    reshape x2 -> x1, local copies, waits for them, and re-layouts: 4.74 us -> 3.19 us  [on_device(): picked_all = bcast(picked_all.reshape(split)).reshape(picked_all.shape)]
where the time goes in v5:
time: 166 us; the launch traced here: 165 us
  Pallas kernels  132 us (80%)
  local copies, waits for them, and re-layouts  15.1 us (9%)
  other arithmetic  14.3 us (9%)
  between operations  2.76 us (2%)
    pallas_call x1, Pallas kernels, bcast(): pl.pallas_call(bcast_kernel, out_shape=jax.ShapeDtypeStruct(shape, jnp.fl...  63.3 us
    pallas_call x1, Pallas kernels, win_sum(): pl.pallas_call(win_sum_kernel, out_shape=jax.ShapeDtypeStruct((rows, cols...  57.5 us
    pallas_call x1, Pallas kernels, correlate_all(): pl.pallas_call(functools.partial(corr_kernel, scale), grid=(steps,), in_s...  11.5 us
    sin x2, other arithmetic, lag_factors(): return (jnp.cos(a), jnp.sin(a), jnp.cos(b), jnp.sin(b))  9.19 us
    reshape x2, local copies, waits for them, and re-layouts, on_device(): return win_sum(stacked.reshape(-1, NLAG)).reshape(stacked.shape)  4.31 us
    gather x4, local copies, waits for them, and re-layouts, on_device(): block = jnp.take(weighted, source_slots[step], axis=1)  3.61 us

profile of v5, /device:TPU:1, one launch (start us, length us, event | category | flops | bytes accessed | tf_op | source)
XLA Modules:
  0.0 164.5 jit_solution(6599451664849910498)
XLA Ops:
  0.0 0.7 convert_element_type.13
  0.7 1.5 fusion.11
  4.7 0.8 compare_and_fusion.3
  5.7 1.2 multiply_reduce_fusion
  6.9 0.1 reduce_sum.14
  7.1 0.1 reduce_sum.18
  7.4 0.2 divide_multiply_fusion
  7.6 0.9 gather_fusion.3
  8.5 0.9 gather_fusion.2
  9.4 0.4 bitcast_select_fusion
  9.8 0.1 copy.20
  9.9 0.2 stack.18
  10.1 0.9 gather_fusion.1
  11.0 0.9 gather_fusion
  11.9 0.4 bitcast_select_fusion.2
  12.3 0.1 copy.18
  12.5 0.2 stack.16
  12.6 0.1 copy.17
  12.8 0.2 stack.15
  12.9 0.1 copy.19
  13.1 0.2 stack.17
  13.2 1.2 pad_maximum_fusion.m_ref
  14.4 63.3 %shard_map.46 = f32[4,8,78,128]{3,2,1,0:T(8,128)} custom-call(f32[4,8,78,128]{3,2,1,0:T(8,128)} %pad_maximum_fusion.m_ref), custom_call_target="tpu_custom_call" | custom-call | tf_op jit(solution)/shard_map/pallas_call | solution.py:238
  77.7 3.2 %reshape.45.src_ref = f32[4,2,4,2,3,1664]{5,4,3,2,1,0:T(4,128)} reshape(f32[4,8,78,128]{3,2,1,0:T(8,128)} %shard_map.46) | data formatting | bytes 2555904 | tf_op jit(solution)/shard_map/reshape | solution.py:276
  80.9 0.8 copy.22.rec_ref
  81.7 0.3 copy.21
  82.0 3.8 %multiply_sine_fusion = (f32[1664,6]{1,0:T(8,128)}, f32[1664,6]{1,0:T(8,128)}) fusion(f32[1664,6]{1,0:T(8,128)S(1)} %copy.21), kind=kLoop, calls=%fused_computation.14 | loop fusion | flops 9984 | bytes 119808 | tf_op jit(solution)/shard_map/sin | solution.py:45
  85.8 5.4 %fusion.4 = (f32[1664,128]{1,0:T(8,128)}, f32[1664,128]{1,0:T(8,128)}) fusion(s32[1664]{0:T(1024)S(1)} %iota_add_fusion), kind=kLoop, calls=%fused_computation.11 | loop fusion | flops 1916928 | bytes 1710592 | tf_op jit(solution)/shard_map/sin | solution.py:45
  91.2 11.5 %shard_map.47 = f32[4,144,768]{2,1,0:T(8,128)} custom-call(f32[4,2,4,2,3,1664]{5,4,3,2,1,0:T(4,128)} %reshape.45.src_ref, f32[2,2,12,1664]{3,2,1,0:T(8,128)} %copy.22.rec_ref, f32[1664,6]{1,0:T(8,128)} %get-tuple-element.15.ca_ref, f32[1664,6]{1,0:T(8,128)} %get-tuple-element.14.sa_ref, f32[1664,128]{1,0:T(8,128)} %get-tuple-element.17.cb_ref, ...), custom_call_target="tpu_custom_call" | custom-call | tf_op jit(solution)/shard_map/pallas_call | solution.py:93
  102.7 57.5 %shard_map.48 = f32[576,768]{1,0:T(8,128)} custom-call(f32[576,768]{1,0:T(8,128)} %bitcast.29), custom_call_target="tpu_custom_call" | custom-call | tf_op jit(solution)/shard_map/pallas_call | solution.py:167
  160.2 2.6 %reshape.47 = f32[4,4,3,4,3,768]{5,4,3,2,1,0:T(4,128)S(1)} reshape(f32[576,768]{1,0:T(8,128)} %shard_map.48) | data formatting | bytes 3538944 | tf_op jit(solution)/shard_map/reshape | solution.py:282
  162.9 1.7 %copy.23 = f32[4,4,3,4,3,768]{5,3,4,2,1,0:T(4,128)} copy(f32[4,4,3,4,3,768]{5,4,3,2,1,0:T(4,128)S(1)} %reshape.47) | data formatting | bytes 3538944 | tf_op jit(solution)/shard_map/reshape | solution.py:282
  (12 shorter events, 0.3 us)
Async XLA Ops:
  0.0 7.4 %copy-start = (f32[2,4,2,3,1664]{4,2,3,1,0:T(2,128)S(1)}, f32[2,4,2,3,1664]{4,2,3,1,0:T(2,128)}, u32[]{:S(2)}) copy-start(f32[2,4,2,3,1664]{4,2,3,1,0:T(2,128)} %param.6) | copy-start | bytes 958468

commit v6 on v5

--- a/solution.py
+++ b/solution.py
@@ -36,12 +36,12 @@
 
 
 def lag_factors(bins, lags):
-    freq = jnp.arange(bins, dtype=jnp.int32) + 360
-    q = jnp.arange(lags // 128, dtype=jnp.int32) * 128 - lags // 2
-    k = jnp.arange(128, dtype=jnp.int32)
+    shift = jnp.arange(lags, dtype=jnp.int32) - lags // 2
+    hi = jnp.arange(bins // 64, dtype=jnp.int32) * 64 + 360
+    lo = jnp.arange(64, dtype=jnp.int32)
     unit = 2.0 * math.pi / 7200.0
-    a = jnp.mod(freq[:, None] * q[None, :], 7200).astype(jnp.float32) * unit
-    b = jnp.mod(freq[:, None] * k[None, :], 7200).astype(jnp.float32) * unit
+    a = jnp.mod(hi[:, None] * shift[None, :], 7200).astype(jnp.float32) * unit
+    b = jnp.mod(lo[:, None] * shift[None, :], 7200).astype(jnp.float32) * unit
     return jnp.cos(a), jnp.sin(a), jnp.cos(b), jnp.sin(b)
 
 
@@ -55,12 +55,13 @@
     def _():
         cb = cb_ref[...]
         sb = sb_ref[...]
-        for q in range(ca_ref.shape[1]):
-            ca = ca_ref[:, pl.ds(q, 1)]
-            sa = sa_ref[:, pl.ds(q, 1)]
-            cols = pl.ds(q * 128, 128)
-            tab_ref[0, :, cols] = ((ca * cb - sa * sb) * scale).astype(jnp.bfloat16)
-            tab_ref[1, :, cols] = (-((sa * cb + ca * sb) * scale)).astype(jnp.bfloat16)
+        step = cb_ref.shape[0]
+        for f1 in range(ca_ref.shape[0]):
+            ca = ca_ref[pl.ds(f1, 1), :]
+            sa = sa_ref[pl.ds(f1, 1), :]
+            rows = pl.ds(f1 * step, step)
+            tab_ref[0, rows, :] = ((ca * cb - sa * sb) * scale).astype(jnp.bfloat16)
+            tab_ref[1, rows, :] = (-((sa * cb + ca * sb) * scale)).astype(jnp.bfloat16)
 
     for s in range(n_src):
         for i in range(n_cmp):

time: 166 us -> 156 us (0.940)
  other arithmetic: 14.3 us -> 7.79 us
  Pallas kernels: 132 us -> 130 us
    sin x2, other arithmetic: 9.19 us -> 2.74 us  [lag_factors(): return (jnp.cos(a), jnp.sin(a), jnp.cos(b), jnp.sin(b))]
    pallas_call x1, Pallas kernels: 11.5 us -> 8.98 us  [correlate_all(): pl.pallas_call(functools.partial(corr_kernel, scale), grid=(steps,), in_s...]
where the time goes in v6:
time: 156 us; the launch traced here: 155 us
  Pallas kernels  130 us (83%)
  local copies, waits for them, and re-layouts  14.6 us (9%)
  other arithmetic  7.79 us (5%)
  between operations  2.74 us (2%)
    pallas_call x1, Pallas kernels, bcast(): pl.pallas_call(bcast_kernel, out_shape=jax.ShapeDtypeStruct(shape, jnp.fl...  63.3 us
    pallas_call x1, Pallas kernels, win_sum(): pl.pallas_call(win_sum_kernel, out_shape=jax.ShapeDtypeStruct((rows, cols...  57.5 us
    pallas_call x1, Pallas kernels, correlate_all(): pl.pallas_call(functools.partial(corr_kernel, scale), grid=(steps,), in_s...  8.98 us
    reshape x2, local copies, waits for them, and re-layouts, on_device(): return win_sum(stacked.reshape(-1, NLAG)).reshape(stacked.shape)  4.31 us
    gather x4, local copies, waits for them, and re-layouts, on_device(): block = jnp.take(weighted, source_slots[step], axis=1)  3.61 us

profile of v6, /device:TPU:1, one launch (start us, length us, event | category | flops | bytes accessed | tf_op | source)
XLA Modules:
  0.0 154.9 jit_solution(1750199349534780957)
XLA Ops:
  0.0 0.7 convert_element_type.13
  0.7 1.5 fusion.14
  4.7 0.8 compare_and_fusion.3
  5.6 1.2 multiply_reduce_fusion
  6.8 0.1 reduce_sum.14
  7.0 0.1 reduce_sum.18
  7.2 0.1 div.22
  7.3 1.2 fusion.11
  8.5 0.2 divide_multiply_fusion
  8.7 0.9 gather_fusion.3
  9.6 0.9 gather_fusion.2
  10.5 0.4 bitcast_select_fusion
  10.9 0.1 copy.14
  11.0 0.2 stack.18
  11.2 0.9 gather_fusion.1
  12.1 0.9 gather_fusion
  13.0 0.4 bitcast_select_fusion.2
  13.4 0.1 copy.12
  13.5 0.2 stack.16
  13.7 1.6 %fusion.4 = (f32[64,768]{1,0:T(8,128)}, f32[64,768]{1,0:T(8,128)}) fusion(s32[768]{0:T(1024)S(1)} %iota_add_fusion), kind=kLoop, calls=%fused_computation.17 | loop fusion | flops 442368 | bytes 396288 | tf_op jit(solution)/shard_map/sin | solution.py:45
  15.3 0.1 copy.11
  15.4 0.2 stack.15
  15.6 0.1 copy.13
  15.7 0.2 stack.17
  15.9 1.2 pad_maximum_fusion.m_ref
  17.0 63.3 %shard_map.46 = f32[4,8,78,128]{3,2,1,0:T(8,128)} custom-call(f32[4,8,78,128]{3,2,1,0:T(8,128)} %pad_maximum_fusion.m_ref), custom_call_target="tpu_custom_call" | custom-call | tf_op jit(solution)/shard_map/pallas_call | solution.py:239
  80.3 3.0 %reshape.45.src_ref = f32[4,2,4,2,3,1664]{5,4,3,2,1,0:T(4,128)} reshape(f32[4,8,78,128]{3,2,1,0:T(8,128)} %shard_map.46) | data formatting | bytes 2555904 | tf_op jit(solution)/shard_map/reshape | solution.py:277
  83.3 0.8 copy.15.rec_ref
  84.1 9.0 %shard_map.47 = f32[4,144,768]{2,1,0:T(8,128)} custom-call(f32[4,2,4,2,3,1664]{5,4,3,2,1,0:T(4,128)} %reshape.45.src_ref, f32[2,2,12,1664]{3,2,1,0:T(8,128)} %copy.15.rec_ref, f32[26,768]{1,0:T(8,128)} %get-tuple-element.15.ca_ref, f32[26,768]{1,0:T(8,128)} %get-tuple-element.14.sa_ref, f32[64,768]{1,0:T(8,128)} %get-tuple-element.17.cb_ref, ...), custom_call_target="tpu_custom_call" | custom-call | tf_op jit(solution)/shard_map/pallas_call | solution.py:94
  93.1 57.5 %shard_map.48 = f32[576,768]{1,0:T(8,128)} custom-call(f32[576,768]{1,0:T(8,128)} %bitcast.29), custom_call_target="tpu_custom_call" | custom-call | tf_op jit(solution)/shard_map/pallas_call | solution.py:168
  150.6 2.6 %reshape.47 = f32[4,4,3,4,3,768]{5,4,3,2,1,0:T(4,128)S(1)} reshape(f32[576,768]{1,0:T(8,128)} %shard_map.48) | data formatting | bytes 3538944 | tf_op jit(solution)/shard_map/reshape | solution.py:283
  153.3 1.7 %copy.16 = f32[4,4,3,4,3,768]{5,3,4,2,1,0:T(4,128)} copy(f32[4,4,3,4,3,768]{5,4,3,2,1,0:T(4,128)S(1)} %reshape.47) | data formatting | bytes 3538944 | tf_op jit(solution)/shard_map/reshape | solution.py:283
  (10 shorter events, 0.1 us)
Async XLA Ops:
  0.0 8.5 %copy-start = (f32[2,4,2,3,1664]{4,2,3,1,0:T(2,128)S(1)}, f32[2,4,2,3,1664]{4,2,3,1,0:T(2,128)}, u32[]{:S(2)}) copy-start(f32[2,4,2,3,1664]{4,2,3,1,0:T(2,128)} %param.6) | copy-start | bytes 958468

commit v7 on v6

--- a/solution.py
+++ b/solution.py
@@ -183,40 +183,54 @@
     )(x)
 
 
-def bcast_kernel(m_ref, out_ref, rx, s1, ry, piece, zr, sx, rxs, sy, rys, agy_s, agy_r, agx_s, agx_r, zsem):
+def bcast_kernel(m_ref, out_ref, rx, s1, ry, piece, zr, rlp, rlm, sx, rxs, sy, rys, agy_s, agy_r, agx_s, agx_r, zsem):
     nx, ny = m_ref.shape[0], m_ref.shape[1]
+    hy = ny // 2
     y, x, zh, zl, c = (lax.axis_index(a) for a in STA + WIN)
-    xpeer = lambda p: (y, p, zh, zl, c)
+    xpeer = lambda p: (y, p % nx, zh, zl, c)
     ypeer = lambda p: (p, x, zh, zl, c)
     zpeer = (y, x, 1 - zh, zl, c)
+    up, down = (x + 1) % nx, (x + nx - 1) % nx
+    far = (x + 2) % nx
 
     barrier = pltpu.get_barrier_semaphore()
-    for d in range(1, nx):
-        pl.semaphore_signal(barrier, inc=1, device_id=xpeer((x + d) % nx), device_id_type=MESH_ID)
+    for p in (up, down):
+        pl.semaphore_signal(barrier, inc=1, device_id=xpeer(p), device_id_type=MESH_ID)
     for d in range(1, ny):
         pl.semaphore_signal(barrier, inc=1, device_id=ypeer((y + d) % ny), device_id_type=MESH_ID)
     pl.semaphore_signal(barrier, inc=1, device_id=zpeer, device_id_type=MESH_ID)
-    pl.semaphore_wait(barrier, nx + ny - 1)
-
-    def send_all(n, me, peer, src, dst, ssem, rsem):
-        copies = []
-        for d in range(1, n):
-            to = (me + d) % n
-            cp = pltpu.make_async_remote_copy(
-                src_ref=src(to), dst_ref=dst, send_sem=ssem.at[d], recv_sem=rsem.at[d],
-                device_id=peer(to), device_id_type=MESH_ID)
-            cp.start()
-            copies.append(cp)
-        for cp in copies:
-            cp.wait()
-
-    send_all(nx, x, xpeer, lambda to: m_ref.at[to], rx.at[x], sx, rxs)
-    total = m_ref[x]
-    for d in range(1, nx):
-        total = total + rx[(x + nx - d) % nx]
-    s1[...] = total
-
-    send_all(ny, y, ypeer, lambda to: s1.at[to], ry.at[y], sy, rys)
+    pl.semaphore_wait(barrier, ny + 2)
+
+    def remote(src, dst, ssem, rsem, k, peer):
+        cp = pltpu.make_async_remote_copy(
+            src_ref=src, dst_ref=dst, send_sem=ssem.at[k], recv_sem=rsem.at[k],
+            device_id=peer, device_id_type=MESH_ID)
+        cp.start()
+        return cp
+
+    lo, hi = pl.ds(0, hy), pl.ds(hy, ny - hy)
+    first = [
+        remote(m_ref.at[up], rx.at[x], sx, rxs, 0, xpeer(up)),
+        remote(m_ref.at[down], rx.at[x], sx, rxs, 1, xpeer(down)),
+        remote(m_ref.at[far, lo], rlp, sx, rxs, 2, xpeer(up)),
+        remote(m_ref.at[far, hi], rlm, sx, rxs, 3, xpeer(down)),
+    ]
+    for cp in first:
+        cp.wait()
+    second = [
+        remote(rlp, rx.at[down, lo], sx, rxs, 4, xpeer(up)),
+        remote(rlm, rx.at[up, hi], sx, rxs, 5, xpeer(down)),
+    ]
+    for cp in second:
+        cp.wait()
+    s1[...] = m_ref[x] + rx[up] + rx[down] + rx[far]
+
+    copies = []
+    for d in range(1, ny):
+        to = (y + d) % ny
+        copies.append(remote(s1.at[to], ry.at[y], sy, rys, d, ypeer(to)))
+    for cp in copies:
+        cp.wait()
     part = s1[y]
     for d in range(1, ny):
         part = part + ry[(y + ny - d) % ny]
@@ -229,8 +243,25 @@
     cp.wait()
     out_ref[x, y] = piece[...] + zr[...]
 
-    send_all(ny, y, ypeer, lambda to: out_ref.at[x, y], out_ref.at[x, y], agy_s, agy_r)
-    send_all(nx, x, xpeer, lambda to: out_ref.at[x], out_ref.at[x], agx_s, agx_r)
+    copies = []
+    for d in range(1, ny):
+        to = (y + d) % ny
+        copies.append(remote(out_ref.at[x, y], out_ref.at[x, y], agy_s, agy_r, d, ypeer(to)))
+    for cp in copies:
+        cp.wait()
+
+    first = [
+        remote(out_ref.at[x], out_ref.at[x], agx_s, agx_r, 0, xpeer(up)),
+        remote(out_ref.at[x], out_ref.at[x], agx_s, agx_r, 1, xpeer(down)),
+    ]
+    for cp in first:
+        cp.wait()
+    second = [
+        remote(out_ref.at[down, lo], out_ref.at[down, lo], agx_s, agx_r, 2, xpeer(up)),
+        remote(out_ref.at[up, hi], out_ref.at[up, hi], agx_s, agx_r, 3, xpeer(down)),
+    ]
+    for cp in second:
+        cp.wait()
 
 
 def bcast(masked):
@@ -247,14 +278,16 @@
             pltpu.VMEM(shape[1:], jnp.float32),
             pltpu.VMEM(shape[2:], jnp.float32),
             pltpu.VMEM(shape[2:], jnp.float32),
-            pltpu.SemaphoreType.DMA((nx,)),
-            pltpu.SemaphoreType.DMA((nx,)),
+            pltpu.VMEM((shape[1] // 2,) + shape[2:], jnp.float32),
+            pltpu.VMEM((shape[1] - shape[1] // 2,) + shape[2:], jnp.float32),
+            pltpu.SemaphoreType.DMA((6,)),
+            pltpu.SemaphoreType.DMA((6,)),
             pltpu.SemaphoreType.DMA((ny,)),
             pltpu.SemaphoreType.DMA((ny,)),
             pltpu.SemaphoreType.DMA((ny,)),
             pltpu.SemaphoreType.DMA((ny,)),
-            pltpu.SemaphoreType.DMA((nx,)),
-            pltpu.SemaphoreType.DMA((nx,)),
+            pltpu.SemaphoreType.DMA((4,)),
+            pltpu.SemaphoreType.DMA((4,)),
             pltpu.SemaphoreType.DMA((2,)),
         ],
         compiler_params=pltpu.CompilerParams(collective_id=1, has_side_effects=True),

time: 156 us -> 156 us (level)
  no operation moved by 1% of the time
where the time goes in v7:
time: 156 us; the launch traced here: 155 us
  Pallas kernels  130 us (83%)
  local copies, waits for them, and re-layouts  14.6 us (9%)
  other arithmetic  7.79 us (5%)
  between operations  2.74 us (2%)
    pallas_call x1, Pallas kernels, bcast(): pl.pallas_call(bcast_kernel, out_shape=jax.ShapeDtypeStruct(shape, jnp.fl...  62.5 us
    pallas_call x1, Pallas kernels, win_sum(): pl.pallas_call(win_sum_kernel, out_shape=jax.ShapeDtypeStruct((rows, cols...  58.5 us
    pallas_call x1, Pallas kernels, correlate_all(): pl.pallas_call(functools.partial(corr_kernel, scale), grid=(steps,), in_s...  8.98 us
    reshape x2, local copies, waits for them, and re-layouts, on_device(): return win_sum(stacked.reshape(-1, NLAG)).reshape(stacked.shape)  4.31 us
    gather x4, local copies, waits for them, and re-layouts, on_device(): block = jnp.take(weighted, source_slots[step], axis=1)  3.61 us

profile of v7, /device:TPU:1, one launch (start us, length us, event | category | flops | bytes accessed | tf_op | source)
XLA Modules:
  0.0 155.1 jit_solution(6248628465662430013)
XLA Ops:
  0.0 0.7 convert_element_type.13
  0.7 1.5 fusion.14
  4.7 0.8 compare_and_fusion.3
  5.6 1.2 multiply_reduce_fusion
  6.8 0.1 reduce_sum.14
  7.0 0.1 reduce_sum.18
  7.2 0.1 div.22
  7.3 1.2 fusion.11
  8.5 0.2 divide_multiply_fusion
  8.7 0.9 gather_fusion.3
  9.6 0.9 gather_fusion.2
  10.5 0.4 bitcast_select_fusion
  10.9 0.1 copy.14
  11.0 0.2 stack.18
  11.2 0.9 gather_fusion.1
  12.1 0.9 gather_fusion
  13.0 0.4 bitcast_select_fusion.2
  13.4 0.1 copy.12
  13.5 0.2 stack.16
  13.7 1.6 %fusion.4 = (f32[64,768]{1,0:T(8,128)}, f32[64,768]{1,0:T(8,128)}) fusion(s32[768]{0:T(1024)S(1)} %iota_add_fusion), kind=kLoop, calls=%fused_computation.17 | loop fusion | flops 442368 | bytes 396288 | tf_op jit(solution)/shard_map/sin | solution.py:45
  15.3 0.1 copy.11
  15.4 0.2 stack.15
  15.6 0.1 copy.13
  15.7 0.2 stack.17
  15.9 1.2 pad_maximum_fusion.m_ref
  17.0 62.5 %shard_map.46 = f32[4,8,78,128]{3,2,1,0:T(8,128)} custom-call(f32[4,8,78,128]{3,2,1,0:T(8,128)} %pad_maximum_fusion.m_ref), custom_call_target="tpu_custom_call" | custom-call | tf_op jit(solution)/shard_map/pallas_call | solution.py:270
  79.5 3.0 %reshape.45.src_ref = f32[4,2,4,2,3,1664]{5,4,3,2,1,0:T(4,128)} reshape(f32[4,8,78,128]{3,2,1,0:T(8,128)} %shard_map.46) | data formatting | bytes 2555904 | tf_op jit(solution)/shard_map/reshape | solution.py:310
  82.5 0.8 copy.15.rec_ref
  83.3 9.0 %shard_map.47 = f32[4,144,768]{2,1,0:T(8,128)} custom-call(f32[4,2,4,2,3,1664]{5,4,3,2,1,0:T(4,128)} %reshape.45.src_ref, f32[2,2,12,1664]{3,2,1,0:T(8,128)} %copy.15.rec_ref, f32[26,768]{1,0:T(8,128)} %get-tuple-element.15.ca_ref, f32[26,768]{1,0:T(8,128)} %get-tuple-element.14.sa_ref, f32[64,768]{1,0:T(8,128)} %get-tuple-element.17.cb_ref, ...), custom_call_target="tpu_custom_call" | custom-call | tf_op jit(solution)/shard_map/pallas_call | solution.py:94
  92.3 58.5 %shard_map.48 = f32[576,768]{1,0:T(8,128)} custom-call(f32[576,768]{1,0:T(8,128)} %bitcast.29), custom_call_target="tpu_custom_call" | custom-call | tf_op jit(solution)/shard_map/pallas_call | solution.py:168
  150.8 2.6 %reshape.47 = f32[4,4,3,4,3,768]{5,4,3,2,1,0:T(4,128)S(1)} reshape(f32[576,768]{1,0:T(8,128)} %shard_map.48) | data formatting | bytes 3538944 | tf_op jit(solution)/shard_map/reshape | solution.py:316
  153.5 1.7 %copy.16 = f32[4,4,3,4,3,768]{5,3,4,2,1,0:T(4,128)} copy(f32[4,4,3,4,3,768]{5,4,3,2,1,0:T(4,128)S(1)} %reshape.47) | data formatting | bytes 3538944 | tf_op jit(solution)/shard_map/reshape | solution.py:316
  (10 shorter events, 0.1 us)
Async XLA Ops:
  0.0 8.5 %copy-start = (f32[2,4,2,3,1664]{4,2,3,1,0:T(2,128)S(1)}, f32[2,4,2,3,1664]{4,2,3,1,0:T(2,128)}, u32[]{:S(2)}) copy-start(f32[2,4,2,3,1664]{4,2,3,1,0:T(2,128)} %param.6) | copy-start | bytes 958468

commit v8 on v6

--- a/solution.py
+++ b/solution.py
@@ -268,11 +268,11 @@
     n_win = lax.axis_size(WIN)
     factors = lag_factors(bins, NLAG)
     me = lax.axis_index(STA)
-    chosen = []
-    for step in range(STEPS):
-        block = jnp.take(weighted, source_slots[step], axis=1)
-        chosen.append(jnp.where(me == owners[step], block, 0.0))
-    picked_all = jnp.stack(chosen)
+    slots = source_slots[:, None, :, None, None, None]
+    picked_all = jnp.zeros((STEPS,) + weighted.shape, weighted.dtype)
+    for k in range(weighted.shape[1]):
+        picked_all = jnp.where(slots == k, weighted[None, :, k : k + 1], picked_all)
+    picked_all = jnp.where((me == owners)[:, None, None, None, None, None], picked_all, 0.0)
     split = (lax.axis_size("x"), lax.axis_size("y"), -1, 128)
     picked_all = bcast(picked_all.reshape(split)).reshape(picked_all.shape)
     shape = weighted.shape

time: 156 us -> 149 us (0.955)
  local copies, waits for them, and re-layouts: 14.6 us -> 10.3 us
  between operations: 2.74 us -> 0.17 us
    gather x4 -> x0, local copies, waits for them, and re-layouts: 3.61 us -> none  [on_device(): block = jnp.take(weighted, source_slots[step], axis=1)]
where the time goes in v8:
time: 149 us; the launch traced here: 148 us
  Pallas kernels  130 us (87%)
  local copies, waits for them, and re-layouts  10.3 us (7%)
  other arithmetic  7.75 us (5%)
    pallas_call x1, Pallas kernels, bcast(): pl.pallas_call(bcast_kernel, out_shape=jax.ShapeDtypeStruct(shape, jnp.fl...  63.3 us
    pallas_call x1, Pallas kernels, win_sum(): pl.pallas_call(win_sum_kernel, out_shape=jax.ShapeDtypeStruct((rows, cols...  57.5 us
    pallas_call x1, Pallas kernels, correlate_all(): pl.pallas_call(functools.partial(corr_kernel, scale), grid=(steps,), in_s...  8.98 us
    reshape x2, local copies, waits for them, and re-layouts, on_device(): return win_sum(stacked.reshape(-1, NLAG)).reshape(stacked.shape)  4.31 us
    reshape x1, local copies, waits for them, and re-layouts, on_device(): picked_all = bcast(picked_all.reshape(split)).reshape(picked_all.shape)  3 us

profile of v8, /device:TPU:1, one launch (start us, length us, event | category | flops | bytes accessed | tf_op | source)
XLA Modules:
  0.0 148.0 jit_solution(7695177252578116535)
XLA Ops:
  0.0 0.7 broadcast_compare_fusion.4
  0.7 0.7 convert_element_type.13
  1.4 0.7 broadcast_compare_fusion.3
  2.1 0.1 copy.19
  2.2 0.1 copy.20
  2.3 0.1 copy.22
  2.4 0.1 copy.23
  2.5 0.1 copy.28
  2.6 0.1 copy.29
  2.7 0.1 copy.25
  2.8 0.1 copy.26
  2.9 1.2 multiply_reduce_fusion
  4.1 0.1 reduce_sum.14
  4.3 0.1 reduce_sum.18
  4.4 0.1 div.21
  4.5 0.1 div.22
  4.6 1.2 fusion.11
  5.8 0.2 divide_multiply_fusion
  6.2 0.2 broadcast_in_dim.124
  6.5 0.2 broadcast_in_dim.131
  6.6 0.1 broadcast_in_dim.137
  6.7 0.2 broadcast_in_dim.138
  7.0 0.2 broadcast_in_dim.117
  7.1 1.4 select_select_fusion.m_ref
  8.5 63.3 %shard_map.46 = f32[4,8,78,128]{3,2,1,0:T(8,128)} custom-call(f32[4,8,78,128]{3,2,1,0:T(8,128)} %select_select_fusion.m_ref), custom_call_target="tpu_custom_call" | custom-call | tf_op jit(solution)/shard_map/pallas_call | solution.py:239
  71.8 1.6 %fusion.4 = (f32[64,768]{1,0:T(8,128)}, f32[64,768]{1,0:T(8,128)}) fusion(s32[768]{0:T(1024)S(1)} %iota_add_fusion), kind=kLoop, calls=%fused_computation.9 | loop fusion | flops 442368 | bytes 396288 | tf_op jit(solution)/shard_map/sin | solution.py:45
  73.4 3.0 %reshape.53.src_ref = f32[4,2,4,2,3,1664]{5,4,3,2,1,0:T(4,128)} reshape(f32[4,8,78,128]{3,2,1,0:T(8,128)} %shard_map.46) | data formatting | bytes 2555904 | tf_op jit(solution)/shard_map/reshape | solution.py:277
  76.4 0.8 copy.31.rec_ref
  77.2 9.0 %shard_map.47 = f32[4,144,768]{2,1,0:T(8,128)} custom-call(f32[4,2,4,2,3,1664]{5,4,3,2,1,0:T(4,128)} %reshape.53.src_ref, f32[2,2,12,1664]{3,2,1,0:T(8,128)} %copy.31.rec_ref, f32[26,768]{1,0:T(8,128)} %get-tuple-element.10.ca_ref, f32[26,768]{1,0:T(8,128)} %get-tuple-element.9.sa_ref, f32[64,768]{1,0:T(8,128)} %get-tuple-element.12.cb_ref, ...), custom_call_target="tpu_custom_call" | custom-call | tf_op jit(solution)/shard_map/pallas_call | solution.py:94
  86.2 57.5 %shard_map.48 = f32[576,768]{1,0:T(8,128)} custom-call(f32[576,768]{1,0:T(8,128)} %bitcast.16), custom_call_target="tpu_custom_call" | custom-call | tf_op jit(solution)/shard_map/pallas_call | solution.py:168
  143.7 2.6 %reshape.55 = f32[4,4,3,4,3,768]{5,4,3,2,1,0:T(4,128)S(1)} reshape(f32[576,768]{1,0:T(8,128)} %shard_map.48) | data formatting | bytes 3538944 | tf_op jit(solution)/shard_map/reshape | solution.py:283
  146.4 1.7 %copy.32 = f32[4,4,3,4,3,768]{5,3,4,2,1,0:T(4,128)} copy(f32[4,4,3,4,3,768]{5,4,3,2,1,0:T(4,128)S(1)} %reshape.55) | data formatting | bytes 3538944 | tf_op jit(solution)/shard_map/reshape | solution.py:283
  (17 shorter events, 0.4 us)
Async XLA Ops:
  0.0 5.8 %copy-start = (f32[2,4,2,3,1664]{4,2,3,1,0:T(2,128)S(1)}, f32[2,4,2,3,1664]{4,2,3,1,0:T(2,128)}, u32[]{:S(2)}) copy-start(f32[2,4,2,3,1664]{4,2,3,1,0:T(2,128)} %param.4) | copy-start | bytes 958468

commit v9 on v8

--- a/solution.py
+++ b/solution.py
@@ -46,9 +46,9 @@
 
 
 def corr_kernel(scale, src_ref, rec_ref, ca_ref, sa_ref, cb_ref, sb_ref, out_ref, rows_ref, tab_ref):
-    n_win = src_ref.shape[1]
-    n_src = src_ref.shape[2]
-    n_cmp = src_ref.shape[4]
+    n_win = rec_ref.shape[0]
+    n_src = src_ref.shape[1] // n_win
+    n_cmp = src_ref.shape[2] // 2
     n_rows = rec_ref.shape[2]
 
     @pl.when(pl.program_id(0) == 0)
@@ -68,8 +68,8 @@
             acc_re = None
             acc_im = None
             for w in range(n_win):
-                sre = src_ref[0, w, s, 0, pl.ds(i, 1), :]
-                sim = src_ref[0, w, s, 1, pl.ds(i, 1), :]
+                sre = src_ref[0, w * n_src + s, pl.ds(i, 1), :]
+                sim = src_ref[0, w * n_src + s, pl.ds(n_cmp + i, 1), :]
                 rre = rec_ref[w, 0]
                 rim = rec_ref[w, 1]
                 re = sre * rre + sim * rim
@@ -85,7 +85,9 @@
 
 
 def correlate_all(picked_all, rec, factors, windows):
-    steps, n_win, n_src, _, n_cmp, bins = picked_all.shape
+    steps, n_ws, n_ri, bins = picked_all.shape
+    n_win = rec.shape[0]
+    n_src, n_cmp = n_ws // n_win, n_ri // 2
     n_rows = rec.shape[2]
     lags = NLAG
     m = n_src * n_cmp * n_rows
@@ -95,7 +97,7 @@
         functools.partial(corr_kernel, scale),
         grid=(steps,),
         in_specs=[
-            pl.BlockSpec((1, n_win, n_src, 2, n_cmp, bins), lambda t: (t, 0, 0, 0, 0, 0)),
+            pl.BlockSpec((1, n_ws, n_ri, bins), lambda t: (t, 0, 0, 0)),
             pl.BlockSpec(rec.shape, lambda t: (0, 0, 0, 0)),
         ]
         + [pl.BlockSpec(f.shape, whole) for f in factors],
@@ -273,8 +275,10 @@
     for k in range(weighted.shape[1]):
         picked_all = jnp.where(slots == k, weighted[None, :, k : k + 1], picked_all)
     picked_all = jnp.where((me == owners)[:, None, None, None, None, None], picked_all, 0.0)
-    split = (lax.axis_size("x"), lax.axis_size("y"), -1, 128)
-    picked_all = bcast(picked_all.reshape(split)).reshape(picked_all.shape)
+    shape6 = picked_all.shape
+    split = (lax.axis_size("x"), lax.axis_size("y"), -1, shape6[-1])
+    rows = (STEPS, shape6[1] * shape6[2], shape6[3] * shape6[4], shape6[5])
+    picked_all = bcast(picked_all.reshape(split)).reshape(rows)
     shape = weighted.shape
     rec = weighted.transpose(0, 2, 1, 3, 4).reshape(shape[0], 2, shape[1] * shape[3], shape[4])
     stacked = correlate_all(picked_all, rec, factors, win_count * n_win).reshape(

time: 149 us -> 164 us (1.10)
  Pallas kernels: 130 us -> 147 us
  local copies, waits for them, and re-layouts: 10.3 us -> 7.48 us
    pallas_call x1, Pallas kernels: 63.3 us -> 79.9 us  [bcast(): pl.pallas_call(bcast_kernel, out_shape=jax.ShapeDtypeStruct(shape, jnp.fl...]
    reshape x1 -> x0, local copies, waits for them, and re-layouts: 3 us -> none  [on_device(): picked_all = bcast(picked_all.reshape(split)).reshape(picked_all.shape)]
where the time goes in v9:
time: 164 us; the launch traced here: 163 us
  Pallas kernels  147 us (90%)
  other arithmetic  8.89 us (5%)
  local copies, waits for them, and re-layouts  7.48 us (5%)
    pallas_call x1, Pallas kernels, bcast(): pl.pallas_call(bcast_kernel, out_shape=jax.ShapeDtypeStruct(shape, jnp.fl...  79.9 us
    pallas_call x1, Pallas kernels, win_sum(): pl.pallas_call(win_sum_kernel, out_shape=jax.ShapeDtypeStruct((rows, cols...  57.2 us
    pallas_call x1, Pallas kernels, correlate_all(): pl.pallas_call(functools.partial(corr_kernel, scale), grid=(steps,), in_s...  9.49 us
    reshape x2, local copies, waits for them, and re-layouts, on_device(): return win_sum(stacked.reshape(-1, NLAG)).reshape(stacked.shape)  4.31 us

profile of v9, /device:TPU:1, one launch (start us, length us, event | category | flops | bytes accessed | tf_op | source)
XLA Modules:
  0.0 163.2 jit_solution(11861436260906746326)
XLA Ops:
  0.0 0.7 broadcast_compare_fusion.4
  0.7 0.7 convert_element_type.13
  1.3 0.7 broadcast_compare_fusion.3
  2.0 0.1 copy.19
  2.1 0.1 copy.20
  2.2 0.1 copy.23
  2.4 0.1 copy.24
  2.5 0.1 copy.31
  2.6 0.1 copy.32
  2.7 0.1 copy.27
  2.8 0.1 copy.28
  2.9 1.2 multiply_reduce_fusion
  4.1 0.1 reduce_sum.14
  4.2 0.1 reduce_sum.18
  4.3 0.1 div.21
  4.4 0.1 div.22
  4.6 1.2 fusion.11
  5.7 1.1 divide_multiply_fusion
  7.2 0.1 broadcast_in_dim.124
  7.4 0.1 broadcast_in_dim.131
  7.7 0.1 broadcast_in_dim.138
  7.8 0.1 copy.34
  8.0 0.1 broadcast_in_dim.117
  8.1 0.1 copy.22
  8.2 1.7 %select_select_fusion.m_ref = f32[4,8,6,1664]{3,2,1,0:T(8,128)} fusion(f32[8,6,1664]{2,1,0:T(8,128)S(1)} %copy.34, f32[8,6,1664]{2,1,0:T(8,128)S(1)} %copy.30, f32[8,6,1664]{2,1,0:T(8,128)S(1)} %copy.26, f32[8,6,1664]{2,1,0:T(8,128)S(1)} %copy.22, pred[4]{0:T(512)(128)(4,1)S(1)} %broadcast_compare_fusion.4, pred[4,8]{1,0:T(4,128)(4,1)S(1)} %copy.32, ...), kind=kLoop, calls=%fused_computation | loop fusion | flops 1597440 | bytes 2556036 | tf_op jit(solution)/shard_map/jit(_where)/select_n | solution.py:277
  9.9 79.9 %shard_map.46.src_ref = f32[4,8,6,1664]{3,2,1,0:T(8,128)} custom-call(f32[4,8,6,1664]{3,2,1,0:T(8,128)} %select_select_fusion.m_ref), custom_call_target="tpu_custom_call" | custom-call | tf_op jit(solution)/shard_map/pallas_call | solution.py:241
  89.8 1.6 fusion.4
  91.4 0.8 copy.35.rec_ref
  92.2 9.5 %shard_map.47 = f32[4,144,768]{2,1,0:T(8,128)} custom-call(f32[4,8,6,1664]{3,2,1,0:T(8,128)} %shard_map.46.src_ref, f32[2,2,12,1664]{3,2,1,0:T(8,128)} %copy.35.rec_ref, f32[26,768]{1,0:T(8,128)} %get-tuple-element.10.ca_ref, f32[26,768]{1,0:T(8,128)} %get-tuple-element.9.sa_ref, f32[64,768]{1,0:T(8,128)} %get-tuple-element.12.cb_ref, ...), custom_call_target="tpu_custom_call" | custom-call | tf_op jit(solution)/shard_map/pallas_call | solution.py:96
  101.7 57.2 %shard_map.48 = f32[576,768]{1,0:T(8,128)} custom-call(f32[576,768]{1,0:T(8,128)} %bitcast.24), custom_call_target="tpu_custom_call" | custom-call | tf_op jit(solution)/shard_map/pallas_call | solution.py:170
  158.9 2.6 %reshape.51 = f32[4,4,3,4,3,768]{5,4,3,2,1,0:T(4,128)S(1)} reshape(f32[576,768]{1,0:T(8,128)} %shard_map.48) | data formatting | bytes 3538944 | tf_op jit(solution)/shard_map/reshape | solution.py:287
  161.5 1.7 %copy.36 = f32[4,4,3,4,3,768]{5,3,4,2,1,0:T(4,128)} copy(f32[4,4,3,4,3,768]{5,4,3,2,1,0:T(4,128)S(1)} %reshape.51) | data formatting | bytes 3538944 | tf_op jit(solution)/shard_map/reshape | solution.py:287
  (18 shorter events, 0.6 us)

commit v10 on v8

--- a/solution.py
+++ b/solution.py
@@ -12,6 +12,7 @@
 NLAG = 768
 STEPS = 4
 MESH_ID = pl.DeviceIdType.MESH
+WIN_CHUNKS = 3
 STA = ("y", "x", "zh")
 WIN = ("zl", "c")
 
@@ -124,10 +125,27 @@
         pl.semaphore_signal(barrier, inc=1, device_id=peer, device_id_type=MESH_ID)
     pl.semaphore_wait(barrier, 3)
 
-    def copy(src, dst, k, peer):
-        return pltpu.make_async_remote_copy(
-            src_ref=src, dst_ref=dst, send_sem=send_sem.at[k], recv_sem=recv_sem.at[k],
-            device_id=peer, device_id_type=MESH_ID)
+    chunks = send_sem.shape[0] // 6
+    width = x_ref.shape[1] // chunks
+
+    class copy:
+        def __init__(self, src, dst, k, peer):
+            self.parts = [
+                pltpu.make_async_remote_copy(
+                    src_ref=src.at[:, pl.ds(j * width, width)],
+                    dst_ref=dst.at[:, pl.ds(j * width, width)],
+                    send_sem=send_sem.at[k * chunks + j], recv_sem=recv_sem.at[k * chunks + j],
+                    device_id=peer, device_id_type=MESH_ID)
+                for j in range(chunks)
+            ]
+
+        def start(self):
+            for part in self.parts:
+                part.start()
+
+        def wait(self):
+            for part in self.parts:
+                part.wait()
 
     mine1 = pl.multiple_of(c * h, 8)
     other1 = pl.multiple_of((1 - c) * h, 8)
@@ -176,8 +194,8 @@
             pltpu.VMEM((rows // 2, cols), jnp.float32),
             pltpu.VMEM((rows // 4, cols), jnp.float32),
             pltpu.VMEM((rows // 8, cols), jnp.float32),
-            pltpu.SemaphoreType.DMA((6,)),
-            pltpu.SemaphoreType.DMA((6,)),
+            pltpu.SemaphoreType.DMA((6 * WIN_CHUNKS,)),
+            pltpu.SemaphoreType.DMA((6 * WIN_CHUNKS,)),
         ],
         compiler_params=pltpu.CompilerParams(collective_id=0, has_side_effects=True),
     )(x)

time: 149 us -> 149 us (level)
  no operation moved by 1% of the time
where the time goes in v10:
time: 149 us; the launch traced here: 148 us
  Pallas kernels  130 us (87%)
  local copies, waits for them, and re-layouts  10.3 us (7%)
  other arithmetic  7.75 us (5%)
    pallas_call x1, Pallas kernels, bcast(): pl.pallas_call(bcast_kernel, out_shape=jax.ShapeDtypeStruct(shape, jnp.fl...  63.3 us
    pallas_call x1, Pallas kernels, win_sum(): pl.pallas_call(win_sum_kernel, out_shape=jax.ShapeDtypeStruct((rows, cols...  57.7 us
    pallas_call x1, Pallas kernels, correlate_all(): pl.pallas_call(functools.partial(corr_kernel, scale), grid=(steps,), in_s...  8.98 us
    reshape x2, local copies, waits for them, and re-layouts, on_device(): return win_sum(stacked.reshape(-1, NLAG)).reshape(stacked.shape)  4.31 us
    reshape x1, local copies, waits for them, and re-layouts, on_device(): picked_all = bcast(picked_all.reshape(split)).reshape(picked_all.shape)  3 us

profile of v10, /device:TPU:1, one launch (start us, length us, event | category | flops | bytes accessed | tf_op | source)
XLA Modules:
  0.0 148.2 jit_solution(2723336674605785133)
XLA Ops:
  0.0 0.7 broadcast_compare_fusion.4
  0.7 0.7 convert_element_type.13
  1.4 0.7 broadcast_compare_fusion.3
  2.1 0.1 copy.19
  2.2 0.1 copy.20
  2.3 0.1 copy.22
  2.4 0.1 copy.23
  2.5 0.1 copy.28
  2.6 0.1 copy.29
  2.7 0.1 copy.25
  2.8 0.1 copy.26
  2.9 1.2 multiply_reduce_fusion
  4.1 0.1 reduce_sum.14
  4.3 0.1 reduce_sum.18
  4.4 0.1 div.21
  4.5 0.1 div.22
  4.6 1.2 fusion.11
  5.8 0.2 divide_multiply_fusion
  6.2 0.2 broadcast_in_dim.124
  6.5 0.2 broadcast_in_dim.131
  6.6 0.1 broadcast_in_dim.137
  6.7 0.2 broadcast_in_dim.138
  7.0 0.2 broadcast_in_dim.117
  7.1 1.4 select_select_fusion.m_ref
  8.5 63.3 %shard_map.46 = f32[4,8,78,128]{3,2,1,0:T(8,128)} custom-call(f32[4,8,78,128]{3,2,1,0:T(8,128)} %select_select_fusion.m_ref), custom_call_target="tpu_custom_call" | custom-call | tf_op jit(solution)/shard_map/pallas_call | solution.py:257
  71.8 1.6 %fusion.4 = (f32[64,768]{1,0:T(8,128)}, f32[64,768]{1,0:T(8,128)}) fusion(s32[768]{0:T(1024)S(1)} %iota_add_fusion), kind=kLoop, calls=%fused_computation.9 | loop fusion | flops 442368 | bytes 396288 | tf_op jit(solution)/shard_map/sin | solution.py:46
  73.4 3.0 %reshape.53.src_ref = f32[4,2,4,2,3,1664]{5,4,3,2,1,0:T(4,128)} reshape(f32[4,8,78,128]{3,2,1,0:T(8,128)} %shard_map.46) | data formatting | bytes 2555904 | tf_op jit(solution)/shard_map/reshape | solution.py:295
  76.4 0.8 copy.31.rec_ref
  77.2 9.0 %shard_map.47 = f32[4,144,768]{2,1,0:T(8,128)} custom-call(f32[4,2,4,2,3,1664]{5,4,3,2,1,0:T(4,128)} %reshape.53.src_ref, f32[2,2,12,1664]{3,2,1,0:T(8,128)} %copy.31.rec_ref, f32[26,768]{1,0:T(8,128)} %get-tuple-element.10.ca_ref, f32[26,768]{1,0:T(8,128)} %get-tuple-element.9.sa_ref, f32[64,768]{1,0:T(8,128)} %get-tuple-element.12.cb_ref, ...), custom_call_target="tpu_custom_call" | custom-call | tf_op jit(solution)/shard_map/pallas_call | solution.py:95
  86.2 57.7 %shard_map.48 = f32[576,768]{1,0:T(8,128)} custom-call(f32[576,768]{1,0:T(8,128)} %bitcast.16), custom_call_target="tpu_custom_call" | custom-call | tf_op jit(solution)/shard_map/pallas_call | solution.py:186
  143.9 2.6 %reshape.55 = f32[4,4,3,4,3,768]{5,4,3,2,1,0:T(4,128)S(1)} reshape(f32[576,768]{1,0:T(8,128)} %shard_map.48) | data formatting | bytes 3538944 | tf_op jit(solution)/shard_map/reshape | solution.py:301
  146.6 1.7 %copy.32 = f32[4,4,3,4,3,768]{5,3,4,2,1,0:T(4,128)} copy(f32[4,4,3,4,3,768]{5,4,3,2,1,0:T(4,128)S(1)} %reshape.55) | data formatting | bytes 3538944 | tf_op jit(solution)/shard_map/reshape | solution.py:301
  (17 shorter events, 0.4 us)
Async XLA Ops:
  0.0 5.8 %copy-start = (f32[2,4,2,3,1664]{4,2,3,1,0:T(2,128)S(1)}, f32[2,4,2,3,1664]{4,2,3,1,0:T(2,128)}, u32[]{:S(2)}) copy-start(f32[2,4,2,3,1664]{4,2,3,1,0:T(2,128)} %param.4) | copy-start | bytes 958468

commit v11 on v8

--- a/solution.py
+++ b/solution.py
@@ -131,36 +131,43 @@
 
     mine1 = pl.multiple_of(c * h, 8)
     other1 = pl.multiple_of((1 - c) * h, 8)
-    cp = copy(x_ref.at[pl.ds(other1, h)], r1, 0, peer_c)
-    cp.start()
-    cp.wait()
-    a1[...] = x_ref[pl.ds(mine1, h), :] + r1[...]
-
     mine2 = pl.multiple_of(b1 * q, 8)
     other2 = pl.multiple_of((1 - b1) * q, 8)
-    cp = copy(a1.at[pl.ds(other2, q)], r2, 1, peer_1)
-    cp.start()
-    cp.wait()
+    first_c = copy(x_ref.at[pl.ds(other1 + other2, q)], r1.at[pl.ds(other2, q)], 0, peer_c)
+    first_c.start()
+    second_c = copy(x_ref.at[pl.ds(other1 + mine2, q)], r1.at[pl.ds(mine2, q)], 1, peer_c)
+    second_c.start()
+    first_c.wait()
+    a1[pl.ds(other2, q), :] = x_ref[pl.ds(mine1 + other2, q), :] + r1[pl.ds(other2, q), :]
+    up_1 = copy(a1.at[pl.ds(other2, q)], r2, 2, peer_1)
+    up_1.start()
+    second_c.wait()
+    a1[pl.ds(mine2, q), :] = x_ref[pl.ds(mine1 + mine2, q), :] + r1[pl.ds(mine2, q), :]
+    up_1.wait()
     a2[...] = a1[pl.ds(mine2, q), :] + r2[...]
 
     mine3 = pl.multiple_of(b2 * e, 8)
     other3 = pl.multiple_of((1 - b2) * e, 8)
-    cp = copy(a2.at[pl.ds(other3, e)], r3, 2, peer_2)
+    cp = copy(a2.at[pl.ds(other3, e)], r3, 3, peer_2)
     cp.start()
     cp.wait()
     base_q = pl.multiple_of(mine1 + mine2, 8)
     at_e = pl.multiple_of(base_q + mine3, 8)
     out_ref[pl.ds(at_e, e), :] = a2[pl.ds(mine3, e), :] + r3[...]
 
-    cp = copy(out_ref.at[pl.ds(at_e, e)], out_ref.at[pl.ds(at_e, e)], 3, peer_2)
+    cp = copy(out_ref.at[pl.ds(at_e, e)], out_ref.at[pl.ds(at_e, e)], 4, peer_2)
     cp.start()
     cp.wait()
-    cp = copy(out_ref.at[pl.ds(base_q, q)], out_ref.at[pl.ds(base_q, q)], 4, peer_1)
-    cp.start()
-    cp.wait()
-    cp = copy(out_ref.at[pl.ds(mine1, h)], out_ref.at[pl.ds(mine1, h)], 5, peer_c)
-    cp.start()
-    cp.wait()
+    down_c1 = copy(out_ref.at[pl.ds(base_q, q)], out_ref.at[pl.ds(base_q, q)], 5, peer_c)
+    down_c1.start()
+    down_1 = copy(out_ref.at[pl.ds(base_q, q)], out_ref.at[pl.ds(base_q, q)], 6, peer_1)
+    down_1.start()
+    down_1.wait()
+    other_q = pl.multiple_of(mine1 + other2, 8)
+    down_c2 = copy(out_ref.at[pl.ds(other_q, q)], out_ref.at[pl.ds(other_q, q)], 7, peer_c)
+    down_c2.start()
+    down_c1.wait()
+    down_c2.wait()
 
 
 def win_sum(x):
@@ -176,8 +183,8 @@
             pltpu.VMEM((rows // 2, cols), jnp.float32),
             pltpu.VMEM((rows // 4, cols), jnp.float32),
             pltpu.VMEM((rows // 8, cols), jnp.float32),
-            pltpu.SemaphoreType.DMA((6,)),
-            pltpu.SemaphoreType.DMA((6,)),
+            pltpu.SemaphoreType.DMA((8,)),
+            pltpu.SemaphoreType.DMA((8,)),
         ],
         compiler_params=pltpu.CompilerParams(collective_id=0, has_side_effects=True),
     )(x)

time: 149 us -> 148 us (level)
  Pallas kernels: 130 us -> 128 us
where the time goes in v11:
time: 148 us; the launch traced here: 147 us
  Pallas kernels  128 us (86%)
  local copies, waits for them, and re-layouts  10.3 us (7%)
  other arithmetic  7.75 us (5%)
    pallas_call x1, Pallas kernels, bcast(): pl.pallas_call(bcast_kernel, out_shape=jax.ShapeDtypeStruct(shape, jnp.fl...  63.3 us
    pallas_call x1, Pallas kernels, win_sum(): pl.pallas_call(win_sum_kernel, out_shape=jax.ShapeDtypeStruct((rows, cols...  56.2 us
    pallas_call x1, Pallas kernels, correlate_all(): pl.pallas_call(functools.partial(corr_kernel, scale), grid=(steps,), in_s...  8.98 us
    reshape x2, local copies, waits for them, and re-layouts, on_device(): return win_sum(stacked.reshape(-1, NLAG)).reshape(stacked.shape)  4.31 us
    reshape x1, local copies, waits for them, and re-layouts, on_device(): picked_all = bcast(picked_all.reshape(split)).reshape(picked_all.shape)  3 us

profile of v11, /device:TPU:1, one launch (start us, length us, event | category | flops | bytes accessed | tf_op | source)
XLA Modules:
  0.0 146.7 jit_solution(2733304682696605688)
XLA Ops:
  0.0 0.7 broadcast_compare_fusion.4
  0.7 0.7 convert_element_type.13
  1.4 0.7 broadcast_compare_fusion.3
  2.1 0.1 copy.19
  2.2 0.1 copy.20
  2.3 0.1 copy.22
  2.4 0.1 copy.23
  2.5 0.1 copy.28
  2.6 0.1 copy.29
  2.7 0.1 copy.25
  2.8 0.1 copy.26
  2.9 1.2 multiply_reduce_fusion
  4.1 0.1 reduce_sum.14
  4.3 0.1 reduce_sum.18
  4.4 0.1 div.21
  4.5 0.1 div.22
  4.6 1.2 fusion.11
  5.8 0.2 divide_multiply_fusion
  6.2 0.2 broadcast_in_dim.124
  6.5 0.2 broadcast_in_dim.131
  6.6 0.1 broadcast_in_dim.137
  6.7 0.2 broadcast_in_dim.138
  7.0 0.2 broadcast_in_dim.117
  7.1 1.4 select_select_fusion.m_ref
  8.5 63.3 %shard_map.46 = f32[4,8,78,128]{3,2,1,0:T(8,128)} custom-call(f32[4,8,78,128]{3,2,1,0:T(8,128)} %select_select_fusion.m_ref), custom_call_target="tpu_custom_call" | custom-call | tf_op jit(solution)/shard_map/pallas_call | solution.py:246
  71.8 1.6 %fusion.4 = (f32[64,768]{1,0:T(8,128)}, f32[64,768]{1,0:T(8,128)}) fusion(s32[768]{0:T(1024)S(1)} %iota_add_fusion), kind=kLoop, calls=%fused_computation.9 | loop fusion | flops 442368 | bytes 396288 | tf_op jit(solution)/shard_map/sin | solution.py:45
  73.4 3.0 %reshape.53.src_ref = f32[4,2,4,2,3,1664]{5,4,3,2,1,0:T(4,128)} reshape(f32[4,8,78,128]{3,2,1,0:T(8,128)} %shard_map.46) | data formatting | bytes 2555904 | tf_op jit(solution)/shard_map/reshape | solution.py:284
  76.4 0.8 copy.31.rec_ref
  77.2 9.0 %shard_map.47 = f32[4,144,768]{2,1,0:T(8,128)} custom-call(f32[4,2,4,2,3,1664]{5,4,3,2,1,0:T(4,128)} %reshape.53.src_ref, f32[2,2,12,1664]{3,2,1,0:T(8,128)} %copy.31.rec_ref, f32[26,768]{1,0:T(8,128)} %get-tuple-element.10.ca_ref, f32[26,768]{1,0:T(8,128)} %get-tuple-element.9.sa_ref, f32[64,768]{1,0:T(8,128)} %get-tuple-element.12.cb_ref, ...), custom_call_target="tpu_custom_call" | custom-call | tf_op jit(solution)/shard_map/pallas_call | solution.py:94
  86.2 56.2 %shard_map.48 = f32[576,768]{1,0:T(8,128)} custom-call(f32[576,768]{1,0:T(8,128)} %bitcast.16), custom_call_target="tpu_custom_call" | custom-call | tf_op jit(solution)/shard_map/pallas_call | solution.py:175
  142.4 2.6 %reshape.55 = f32[4,4,3,4,3,768]{5,4,3,2,1,0:T(4,128)S(1)} reshape(f32[576,768]{1,0:T(8,128)} %shard_map.48) | data formatting | bytes 3538944 | tf_op jit(solution)/shard_map/reshape | solution.py:290
  145.1 1.7 %copy.32 = f32[4,4,3,4,3,768]{5,3,4,2,1,0:T(4,128)} copy(f32[4,4,3,4,3,768]{5,4,3,2,1,0:T(4,128)S(1)} %reshape.55) | data formatting | bytes 3538944 | tf_op jit(solution)/shard_map/reshape | solution.py:290
  (17 shorter events, 0.4 us)
Async XLA Ops:
  0.0 5.8 %copy-start = (f32[2,4,2,3,1664]{4,2,3,1,0:T(2,128)S(1)}, f32[2,4,2,3,1664]{4,2,3,1,0:T(2,128)}, u32[]{:S(2)}) copy-start(f32[2,4,2,3,1664]{4,2,3,1,0:T(2,128)} %param.4) | copy-start | bytes 958468

commit v12 on v11

--- a/solution.py
+++ b/solution.py
@@ -205,26 +205,36 @@
     pl.semaphore_signal(barrier, inc=1, device_id=zpeer, device_id_type=MESH_ID)
     pl.semaphore_wait(barrier, nx + ny - 1)
 
-    def send_all(n, me, peer, src, dst, ssem, rsem):
-        copies = []
-        for d in range(1, n):
-            to = (me + d) % n
-            cp = pltpu.make_async_remote_copy(
-                src_ref=src(to), dst_ref=dst, send_sem=ssem.at[d], recv_sem=rsem.at[d],
-                device_id=peer(to), device_id_type=MESH_ID)
-            cp.start()
-            copies.append(cp)
-        for cp in copies:
+    def remote(src, dst, ssem, rsem, k, peer):
+        cp = pltpu.make_async_remote_copy(
+            src_ref=src, dst_ref=dst, send_sem=ssem.at[k], recv_sem=rsem.at[k],
+            device_id=peer, device_id_type=MESH_ID)
+        cp.start()
+        return cp
+
+    order = list(range(1, ny)) + [0]
+    rs_x = {}
+    for d in order:
+        row = (y + d) % ny
+        rs_x[d] = [
+            remote(m_ref.at[(x + dx) % nx, row], rx.at[x, row], sx, rxs, d * nx + dx, xpeer((x + dx) % nx))
+            for dx in range(1, nx)
+        ]
+    rs_y = []
+    for d in order:
+        row = (y + d) % ny
+        for cp in rs_x[d]:
             cp.wait()
-
-    send_all(nx, x, xpeer, lambda to: m_ref.at[to], rx.at[x], sx, rxs)
-    total = m_ref[x]
-    for d in range(1, nx):
-        total = total + rx[(x + nx - d) % nx]
-    s1[...] = total
-
-    send_all(ny, y, ypeer, lambda to: s1.at[to], ry.at[y], sy, rys)
-    part = s1[y]
+        total = m_ref[x, row]
+        for dx in range(1, nx):
+            total = total + rx[(x + nx - dx) % nx, row]
+        if d == 0:
+            part = total
+        else:
+            s1[row] = total
+            rs_y.append(remote(s1.at[row], ry.at[y], sy, rys, d, ypeer(row)))
+    for cp in rs_y:
+        cp.wait()
     for d in range(1, ny):
         part = part + ry[(y + ny - d) % ny]
     piece[...] = part
@@ -236,8 +246,16 @@
     cp.wait()
     out_ref[x, y] = piece[...] + zr[...]
 
-    send_all(ny, y, ypeer, lambda to: out_ref.at[x, y], out_ref.at[x, y], agy_s, agy_r)
-    send_all(nx, x, xpeer, lambda to: out_ref.at[x], out_ref.at[x], agx_s, agx_r)
+    ag_y = {d: remote(out_ref.at[x, y], out_ref.at[x, y], agy_s, agy_r, d, ypeer((y + d) % ny)) for d in range(1, ny)}
+    ag_x = []
+    for d in [0] + list(range(1, ny)):
+        if d:
+            ag_y[d].wait()
+        row = (y + ny - d) % ny
+        for dx in range(1, nx):
+            ag_x.append(remote(out_ref.at[x, row], out_ref.at[x, row], agx_s, agx_r, d * nx + dx, xpeer((x + dx) % nx)))
+    for cp in ag_x:
+        cp.wait()
 
 
 def bcast(masked):
@@ -254,14 +272,14 @@
             pltpu.VMEM(shape[1:], jnp.float32),
             pltpu.VMEM(shape[2:], jnp.float32),
             pltpu.VMEM(shape[2:], jnp.float32),
-            pltpu.SemaphoreType.DMA((nx,)),
-            pltpu.SemaphoreType.DMA((nx,)),
+            pltpu.SemaphoreType.DMA((nx * ny,)),
+            pltpu.SemaphoreType.DMA((nx * ny,)),
             pltpu.SemaphoreType.DMA((ny,)),
             pltpu.SemaphoreType.DMA((ny,)),
             pltpu.SemaphoreType.DMA((ny,)),
             pltpu.SemaphoreType.DMA((ny,)),
-            pltpu.SemaphoreType.DMA((nx,)),
-            pltpu.SemaphoreType.DMA((nx,)),
+            pltpu.SemaphoreType.DMA((nx * ny,)),
+            pltpu.SemaphoreType.DMA((nx * ny,)),
             pltpu.SemaphoreType.DMA((2,)),
         ],
         compiler_params=pltpu.CompilerParams(collective_id=1, has_side_effects=True),

time: 148 us -> 137 us (0.926)
  Pallas kernels: 128 us -> 118 us
    pallas_call x1, Pallas kernels: 63.3 us -> 52.6 us  [bcast(): pl.pallas_call(bcast_kernel, out_shape=jax.ShapeDtypeStruct(shape, jnp.fl...]
where the time goes in v12:
time: 137 us; the launch traced here: 136 us
  Pallas kernels  118 us (86%)
  local copies, waits for them, and re-layouts  10.3 us (8%)
  other arithmetic  7.75 us (6%)
    pallas_call x1, Pallas kernels, win_sum(): pl.pallas_call(win_sum_kernel, out_shape=jax.ShapeDtypeStruct((rows, cols...  56.4 us
    pallas_call x1, Pallas kernels, bcast(): pl.pallas_call(bcast_kernel, out_shape=jax.ShapeDtypeStruct(shape, jnp.fl...  52.6 us
    pallas_call x1, Pallas kernels, correlate_all(): pl.pallas_call(functools.partial(corr_kernel, scale), grid=(steps,), in_s...  8.98 us
    reshape x2, local copies, waits for them, and re-layouts, on_device(): return win_sum(stacked.reshape(-1, NLAG)).reshape(stacked.shape)  4.31 us
    reshape x1, local copies, waits for them, and re-layouts, on_device(): picked_all = bcast(picked_all.reshape(split)).reshape(picked_all.shape)  3 us
    sin x2, other arithmetic, lag_factors(): return (jnp.cos(a), jnp.sin(a), jnp.cos(b), jnp.sin(b))  2.76 us

profile of v12, /device:TPU:1, one launch (start us, length us, event | category | flops | bytes accessed | tf_op | source)
XLA Modules:
  0.0 136.2 jit_solution(1162215755851561708)
XLA Ops:
  0.0 0.7 broadcast_compare_fusion.4
  0.7 0.7 convert_element_type.13
  1.4 0.7 broadcast_compare_fusion.3
  2.1 0.1 copy.19
  2.2 0.1 copy.20
  2.3 0.1 copy.22
  2.4 0.1 copy.23
  2.5 0.1 copy.28
  2.6 0.1 copy.29
  2.7 0.1 copy.25
  2.8 0.1 copy.26
  2.9 1.2 multiply_reduce_fusion
  4.1 0.1 reduce_sum.14
  4.3 0.1 reduce_sum.18
  4.4 0.1 div.21
  4.5 0.1 div.22
  4.6 1.2 fusion.11
  5.8 0.2 divide_multiply_fusion
  6.2 0.2 broadcast_in_dim.124
  6.5 0.2 broadcast_in_dim.131
  6.6 0.1 broadcast_in_dim.137
  6.7 0.2 broadcast_in_dim.138
  7.0 0.2 broadcast_in_dim.117
  7.1 1.4 %select_select_fusion.m_ref = f32[4,8,78,128]{3,2,1,0:T(8,128)} fusion(f32[8,78,128]{2,1,0:T(8,128)S(1)} %broadcast_in_dim.138, f32[8,78,128]{2,1,0:T(8,128)S(1)} %broadcast_in_dim.131, f32[8,78,128]{2,1,0:T(8,128)S(1)} %broadcast_in_dim.124, f32[8,78,128]{2,1,0:T(8,128)S(1)} %broadcast_in_dim.117, pred[4]{0:T(512)(128)(4,1)S(1)} %broadcast_compare_fusion.4, ...), kind=kLoop, calls=%fused_computation | loop fusion | flops 1597440 | bytes 2556036 | tf_op jit(solution)/shard_map/jit(_where)/select_n | solution.py:300
  8.5 52.6 %shard_map.46 = f32[4,8,78,128]{3,2,1,0:T(8,128)} custom-call(f32[4,8,78,128]{3,2,1,0:T(8,128)} %select_select_fusion.m_ref), custom_call_target="tpu_custom_call" | custom-call | tf_op jit(solution)/shard_map/pallas_call | solution.py:264
  61.1 1.6 %fusion.4 = (f32[64,768]{1,0:T(8,128)}, f32[64,768]{1,0:T(8,128)}) fusion(s32[768]{0:T(1024)S(1)} %iota_add_fusion), kind=kLoop, calls=%fused_computation.9 | loop fusion | flops 442368 | bytes 396288 | tf_op jit(solution)/shard_map/sin | solution.py:45
  62.7 3.0 %reshape.53.src_ref = f32[4,2,4,2,3,1664]{5,4,3,2,1,0:T(4,128)} reshape(f32[4,8,78,128]{3,2,1,0:T(8,128)} %shard_map.46) | data formatting | bytes 2555904 | tf_op jit(solution)/shard_map/reshape | solution.py:302
  65.7 0.8 copy.31.rec_ref
  66.5 9.0 %shard_map.47 = f32[4,144,768]{2,1,0:T(8,128)} custom-call(f32[4,2,4,2,3,1664]{5,4,3,2,1,0:T(4,128)} %reshape.53.src_ref, f32[2,2,12,1664]{3,2,1,0:T(8,128)} %copy.31.rec_ref, f32[26,768]{1,0:T(8,128)} %get-tuple-element.10.ca_ref, f32[26,768]{1,0:T(8,128)} %get-tuple-element.9.sa_ref, f32[64,768]{1,0:T(8,128)} %get-tuple-element.12.cb_ref, ...), custom_call_target="tpu_custom_call" | custom-call | tf_op jit(solution)/shard_map/pallas_call | solution.py:94
  75.5 56.4 %shard_map.48 = f32[576,768]{1,0:T(8,128)} custom-call(f32[576,768]{1,0:T(8,128)} %bitcast.16), custom_call_target="tpu_custom_call" | custom-call | tf_op jit(solution)/shard_map/pallas_call | solution.py:175
  131.9 2.6 %reshape.55 = f32[4,4,3,4,3,768]{5,4,3,2,1,0:T(4,128)S(1)} reshape(f32[576,768]{1,0:T(8,128)} %shard_map.48) | data formatting | bytes 3538944 | tf_op jit(solution)/shard_map/reshape | solution.py:308
  134.5 1.7 %copy.32 = f32[4,4,3,4,3,768]{5,3,4,2,1,0:T(4,128)} copy(f32[4,4,3,4,3,768]{5,4,3,2,1,0:T(4,128)S(1)} %reshape.55) | data formatting | bytes 3538944 | tf_op jit(solution)/shard_map/reshape | solution.py:308
  (17 shorter events, 0.4 us)
Async XLA Ops:
  0.0 5.8 %copy-start = (f32[2,4,2,3,1664]{4,2,3,1,0:T(2,128)S(1)}, f32[2,4,2,3,1664]{4,2,3,1,0:T(2,128)}, u32[]{:S(2)}) copy-start(f32[2,4,2,3,1664]{4,2,3,1,0:T(2,128)} %param.4) | copy-start | bytes 958468

commit v13 on v12

--- a/solution.py
+++ b/solution.py
@@ -133,41 +133,57 @@
     other1 = pl.multiple_of((1 - c) * h, 8)
     mine2 = pl.multiple_of(b1 * q, 8)
     other2 = pl.multiple_of((1 - b1) * q, 8)
-    first_c = copy(x_ref.at[pl.ds(other1 + other2, q)], r1.at[pl.ds(other2, q)], 0, peer_c)
-    first_c.start()
-    second_c = copy(x_ref.at[pl.ds(other1 + mine2, q)], r1.at[pl.ds(mine2, q)], 1, peer_c)
-    second_c.start()
-    first_c.wait()
-    a1[pl.ds(other2, q), :] = x_ref[pl.ds(mine1 + other2, q), :] + r1[pl.ds(other2, q), :]
-    up_1 = copy(a1.at[pl.ds(other2, q)], r2, 2, peer_1)
-    up_1.start()
-    second_c.wait()
-    a1[pl.ds(mine2, q), :] = x_ref[pl.ds(mine1 + mine2, q), :] + r1[pl.ds(mine2, q), :]
-    up_1.wait()
-    a2[...] = a1[pl.ds(mine2, q), :] + r2[...]
-
     mine3 = pl.multiple_of(b2 * e, 8)
     other3 = pl.multiple_of((1 - b2) * e, 8)
-    cp = copy(a2.at[pl.ds(other3, e)], r3, 3, peer_2)
-    cp.start()
-    cp.wait()
     base_q = pl.multiple_of(mine1 + mine2, 8)
     at_e = pl.multiple_of(base_q + mine3, 8)
-    out_ref[pl.ds(at_e, e), :] = a2[pl.ds(mine3, e), :] + r3[...]
-
-    cp = copy(out_ref.at[pl.ds(at_e, e)], out_ref.at[pl.ds(at_e, e)], 4, peer_2)
-    cp.start()
-    cp.wait()
-    down_c1 = copy(out_ref.at[pl.ds(base_q, q)], out_ref.at[pl.ds(base_q, q)], 5, peer_c)
-    down_c1.start()
-    down_1 = copy(out_ref.at[pl.ds(base_q, q)], out_ref.at[pl.ds(base_q, q)], 6, peer_1)
-    down_1.start()
-    down_1.wait()
-    other_q = pl.multiple_of(mine1 + other2, 8)
-    down_c2 = copy(out_ref.at[pl.ds(other_q, q)], out_ref.at[pl.ds(other_q, q)], 7, peer_c)
-    down_c2.start()
-    down_c1.wait()
-    down_c2.wait()
+    n_chunks = send_sem.shape[0] // 6
+    width = x_ref.shape[1] // n_chunks
+
+    def stages(j):
+        cols = pl.ds(j * width, width)
+        k = 6 * j
+
+        def run(src, dst, i, peer):
+            cp = copy(src, dst, k + i, peer)
+            cp.start()
+            return cp
+
+        cp = run(x_ref.at[pl.ds(other1, h), cols], r1.at[:, cols], 0, peer_c)
+        yield
+        cp.wait()
+        a1[:, cols] = x_ref[pl.ds(mine1, h), cols] + r1[:, cols]
+        cp = run(a1.at[pl.ds(other2, q), cols], r2.at[:, cols], 1, peer_1)
+        yield
+        cp.wait()
+        a2[:, cols] = a1[pl.ds(mine2, q), cols] + r2[:, cols]
+        cp = run(a2.at[pl.ds(other3, e), cols], r3.at[:, cols], 2, peer_2)
+        yield
+        cp.wait()
+        out_ref[pl.ds(at_e, e), cols] = a2[pl.ds(mine3, e), cols] + r3[:, cols]
+        cp = run(out_ref.at[pl.ds(at_e, e), cols], out_ref.at[pl.ds(at_e, e), cols], 3, peer_2)
+        yield
+        cp.wait()
+        cp = run(out_ref.at[pl.ds(base_q, q), cols], out_ref.at[pl.ds(base_q, q), cols], 4, peer_1)
+        yield
+        cp.wait()
+        cp = run(out_ref.at[pl.ds(mine1, h), cols], out_ref.at[pl.ds(mine1, h), cols], 5, peer_c)
+        yield
+        cp.wait()
+
+    live = [stages(j) for j in range(n_chunks)]
+    next(live[0])
+    started = 1
+    while live:
+        if started < len(live):
+            next(live[started])
+            started += 1
+        for g in list(live[:started]):
+            try:
+                next(g)
+            except StopIteration:
+                live.remove(g)
+                started -= 1
 
 
 def win_sum(x):
@@ -183,8 +199,8 @@
             pltpu.VMEM((rows // 2, cols), jnp.float32),
             pltpu.VMEM((rows // 4, cols), jnp.float32),
             pltpu.VMEM((rows // 8, cols), jnp.float32),
-            pltpu.SemaphoreType.DMA((8,)),
-            pltpu.SemaphoreType.DMA((8,)),
+            pltpu.SemaphoreType.DMA((12,)),
+            pltpu.SemaphoreType.DMA((12,)),
         ],
         compiler_params=pltpu.CompilerParams(collective_id=0, has_side_effects=True),
     )(x)

time: 137 us -> 132 us (0.964)
  Pallas kernels: 118 us -> 113 us
    pallas_call x1, Pallas kernels: 56.4 us -> 51.7 us  [win_sum(): pl.pallas_call(win_sum_kernel, out_shape=jax.ShapeDtypeStruct((rows, cols...]
where the time goes in v13:
time: 132 us; the launch traced here: 131 us
  Pallas kernels  113 us (86%)
  local copies, waits for them, and re-layouts  10.3 us (8%)
  other arithmetic  7.75 us (6%)
    pallas_call x1, Pallas kernels, bcast(): pl.pallas_call(bcast_kernel, out_shape=jax.ShapeDtypeStruct(shape, jnp.fl...  52.6 us
    pallas_call x1, Pallas kernels, win_sum(): pl.pallas_call(win_sum_kernel, out_shape=jax.ShapeDtypeStruct((rows, cols...  51.7 us
    pallas_call x1, Pallas kernels, correlate_all(): pl.pallas_call(functools.partial(corr_kernel, scale), grid=(steps,), in_s...  8.98 us
    reshape x2, local copies, waits for them, and re-layouts, on_device(): return win_sum(stacked.reshape(-1, NLAG)).reshape(stacked.shape)  4.31 us
    reshape x1, local copies, waits for them, and re-layouts, on_device(): picked_all = bcast(picked_all.reshape(split)).reshape(picked_all.shape)  3 us
    sin x2, other arithmetic, lag_factors(): return (jnp.cos(a), jnp.sin(a), jnp.cos(b), jnp.sin(b))  2.76 us

profile of v13, /device:TPU:1, one launch (start us, length us, event | category | flops | bytes accessed | tf_op | source)
XLA Modules:
  0.0 131.5 jit_solution(6842917221545069966)
XLA Ops:
  0.0 0.7 broadcast_compare_fusion.4
  0.7 0.7 convert_element_type.13
  1.4 0.7 broadcast_compare_fusion.3
  2.1 0.1 copy.19
  2.2 0.1 copy.20
  2.3 0.1 copy.22
  2.4 0.1 copy.23
  2.5 0.1 copy.28
  2.6 0.1 copy.29
  2.7 0.1 copy.25
  2.8 0.1 copy.26
  2.9 1.2 multiply_reduce_fusion
  4.1 0.1 reduce_sum.14
  4.3 0.1 reduce_sum.18
  4.4 0.1 div.21
  4.5 0.1 div.22
  4.6 1.2 fusion.11
  5.8 0.2 divide_multiply_fusion
  6.2 0.2 broadcast_in_dim.124
  6.5 0.2 broadcast_in_dim.131
  6.6 0.1 broadcast_in_dim.137
  6.7 0.2 broadcast_in_dim.138
  7.0 0.2 broadcast_in_dim.117
  7.1 1.4 %select_select_fusion.m_ref = f32[4,8,78,128]{3,2,1,0:T(8,128)} fusion(f32[8,78,128]{2,1,0:T(8,128)S(1)} %broadcast_in_dim.138, f32[8,78,128]{2,1,0:T(8,128)S(1)} %broadcast_in_dim.131, f32[8,78,128]{2,1,0:T(8,128)S(1)} %broadcast_in_dim.124, f32[8,78,128]{2,1,0:T(8,128)S(1)} %broadcast_in_dim.117, pred[4]{0:T(512)(128)(4,1)S(1)} %broadcast_compare_fusion.4, ...), kind=kLoop, calls=%fused_computation | loop fusion | flops 1597440 | bytes 2556036 | tf_op jit(solution)/shard_map/jit(_where)/select_n | solution.py:316
  8.5 52.6 %shard_map.46 = f32[4,8,78,128]{3,2,1,0:T(8,128)} custom-call(f32[4,8,78,128]{3,2,1,0:T(8,128)} %select_select_fusion.m_ref), custom_call_target="tpu_custom_call" | custom-call | tf_op jit(solution)/shard_map/pallas_call | solution.py:280
  61.1 1.6 %fusion.4 = (f32[64,768]{1,0:T(8,128)}, f32[64,768]{1,0:T(8,128)}) fusion(s32[768]{0:T(1024)S(1)} %iota_add_fusion), kind=kLoop, calls=%fused_computation.9 | loop fusion | flops 442368 | bytes 396288 | tf_op jit(solution)/shard_map/sin | solution.py:45
  62.7 3.0 %reshape.53.src_ref = f32[4,2,4,2,3,1664]{5,4,3,2,1,0:T(4,128)} reshape(f32[4,8,78,128]{3,2,1,0:T(8,128)} %shard_map.46) | data formatting | bytes 2555904 | tf_op jit(solution)/shard_map/reshape | solution.py:318
  65.7 0.8 copy.31.rec_ref
  66.5 9.0 %shard_map.47 = f32[4,144,768]{2,1,0:T(8,128)} custom-call(f32[4,2,4,2,3,1664]{5,4,3,2,1,0:T(4,128)} %reshape.53.src_ref, f32[2,2,12,1664]{3,2,1,0:T(8,128)} %copy.31.rec_ref, f32[26,768]{1,0:T(8,128)} %get-tuple-element.10.ca_ref, f32[26,768]{1,0:T(8,128)} %get-tuple-element.9.sa_ref, f32[64,768]{1,0:T(8,128)} %get-tuple-element.12.cb_ref, ...), custom_call_target="tpu_custom_call" | custom-call | tf_op jit(solution)/shard_map/pallas_call | solution.py:94
  75.5 51.7 %shard_map.48 = f32[576,768]{1,0:T(8,128)} custom-call(f32[576,768]{1,0:T(8,128)} %bitcast.16), custom_call_target="tpu_custom_call" | custom-call | tf_op jit(solution)/shard_map/pallas_call | solution.py:191
  127.1 2.6 %reshape.55 = f32[4,4,3,4,3,768]{5,4,3,2,1,0:T(4,128)S(1)} reshape(f32[576,768]{1,0:T(8,128)} %shard_map.48) | data formatting | bytes 3538944 | tf_op jit(solution)/shard_map/reshape | solution.py:324
  129.8 1.7 %copy.32 = f32[4,4,3,4,3,768]{5,3,4,2,1,0:T(4,128)} copy(f32[4,4,3,4,3,768]{5,4,3,2,1,0:T(4,128)S(1)} %reshape.55) | data formatting | bytes 3538944 | tf_op jit(solution)/shard_map/reshape | solution.py:324
  (17 shorter events, 0.4 us)
Async XLA Ops:
  0.0 5.8 %copy-start = (f32[2,4,2,3,1664]{4,2,3,1,0:T(2,128)S(1)}, f32[2,4,2,3,1664]{4,2,3,1,0:T(2,128)}, u32[]{:S(2)}) copy-start(f32[2,4,2,3,1664]{4,2,3,1,0:T(2,128)} %param.4) | copy-start | bytes 958468

commit v14 on v13

--- a/solution.py
+++ b/solution.py
@@ -199,8 +199,8 @@
             pltpu.VMEM((rows // 2, cols), jnp.float32),
             pltpu.VMEM((rows // 4, cols), jnp.float32),
             pltpu.VMEM((rows // 8, cols), jnp.float32),
-            pltpu.SemaphoreType.DMA((12,)),
-            pltpu.SemaphoreType.DMA((12,)),
+            pltpu.SemaphoreType.DMA((18,)),
+            pltpu.SemaphoreType.DMA((18,)),
         ],
         compiler_params=pltpu.CompilerParams(collective_id=0, has_side_effects=True),
     )(x)

time: 132 us -> 128 us (0.970)
  Pallas kernels: 113 us -> 109 us
    pallas_call x1, Pallas kernels: 51.7 us -> 47.6 us  [win_sum(): pl.pallas_call(win_sum_kernel, out_shape=jax.ShapeDtypeStruct((rows, cols...]
where the time goes in v14:
time: 128 us; the launch traced here: 127 us
  Pallas kernels  109 us (85%)
  local copies, waits for them, and re-layouts  10.3 us (8%)
  other arithmetic  7.75 us (6%)
    pallas_call x1, Pallas kernels, bcast(): pl.pallas_call(bcast_kernel, out_shape=jax.ShapeDtypeStruct(shape, jnp.fl...  52.6 us
    pallas_call x1, Pallas kernels, win_sum(): pl.pallas_call(win_sum_kernel, out_shape=jax.ShapeDtypeStruct((rows, cols...  47.6 us
    pallas_call x1, Pallas kernels, correlate_all(): pl.pallas_call(functools.partial(corr_kernel, scale), grid=(steps,), in_s...  8.98 us
    reshape x2, local copies, waits for them, and re-layouts, on_device(): return win_sum(stacked.reshape(-1, NLAG)).reshape(stacked.shape)  4.31 us
    reshape x1, local copies, waits for them, and re-layouts, on_device(): picked_all = bcast(picked_all.reshape(split)).reshape(picked_all.shape)  3 us
    sin x2, other arithmetic, lag_factors(): return (jnp.cos(a), jnp.sin(a), jnp.cos(b), jnp.sin(b))  2.76 us

profile of v14, /device:TPU:1, one launch (start us, length us, event | category | flops | bytes accessed | tf_op | source)
XLA Modules:
  0.0 127.4 jit_solution(17933733794738369843)
XLA Ops:
  0.0 0.7 broadcast_compare_fusion.4
  0.7 0.7 convert_element_type.13
  1.4 0.7 broadcast_compare_fusion.3
  2.1 0.1 copy.19
  2.2 0.1 copy.20
  2.3 0.1 copy.22
  2.4 0.1 copy.23
  2.5 0.1 copy.28
  2.6 0.1 copy.29
  2.7 0.1 copy.25
  2.8 0.1 copy.26
  2.9 1.2 multiply_reduce_fusion
  4.1 0.1 reduce_sum.14
  4.3 0.1 reduce_sum.18
  4.4 0.1 div.21
  4.5 0.1 div.22
  4.6 1.2 fusion.11
  5.8 0.2 divide_multiply_fusion
  6.2 0.2 broadcast_in_dim.124
  6.5 0.2 broadcast_in_dim.131
  6.6 0.1 broadcast_in_dim.137
  6.7 0.2 broadcast_in_dim.138
  7.0 0.2 broadcast_in_dim.117
  7.1 1.4 %select_select_fusion.m_ref = f32[4,8,78,128]{3,2,1,0:T(8,128)} fusion(f32[8,78,128]{2,1,0:T(8,128)S(1)} %broadcast_in_dim.138, f32[8,78,128]{2,1,0:T(8,128)S(1)} %broadcast_in_dim.131, f32[8,78,128]{2,1,0:T(8,128)S(1)} %broadcast_in_dim.124, f32[8,78,128]{2,1,0:T(8,128)S(1)} %broadcast_in_dim.117, pred[4]{0:T(512)(128)(4,1)S(1)} %broadcast_compare_fusion.4, ...), kind=kLoop, calls=%fused_computation | loop fusion | flops 1597440 | bytes 2556036 | tf_op jit(solution)/shard_map/jit(_where)/select_n | solution.py:316
  8.5 52.6 %shard_map.46 = f32[4,8,78,128]{3,2,1,0:T(8,128)} custom-call(f32[4,8,78,128]{3,2,1,0:T(8,128)} %select_select_fusion.m_ref), custom_call_target="tpu_custom_call" | custom-call | tf_op jit(solution)/shard_map/pallas_call | solution.py:280
  61.1 1.6 %fusion.4 = (f32[64,768]{1,0:T(8,128)}, f32[64,768]{1,0:T(8,128)}) fusion(s32[768]{0:T(1024)S(1)} %iota_add_fusion), kind=kLoop, calls=%fused_computation.9 | loop fusion | flops 442368 | bytes 396288 | tf_op jit(solution)/shard_map/sin | solution.py:45
  62.7 3.0 %reshape.53.src_ref = f32[4,2,4,2,3,1664]{5,4,3,2,1,0:T(4,128)} reshape(f32[4,8,78,128]{3,2,1,0:T(8,128)} %shard_map.46) | data formatting | bytes 2555904 | tf_op jit(solution)/shard_map/reshape | solution.py:318
  65.7 0.8 copy.31.rec_ref
  66.5 9.0 %shard_map.47 = f32[4,144,768]{2,1,0:T(8,128)} custom-call(f32[4,2,4,2,3,1664]{5,4,3,2,1,0:T(4,128)} %reshape.53.src_ref, f32[2,2,12,1664]{3,2,1,0:T(8,128)} %copy.31.rec_ref, f32[26,768]{1,0:T(8,128)} %get-tuple-element.10.ca_ref, f32[26,768]{1,0:T(8,128)} %get-tuple-element.9.sa_ref, f32[64,768]{1,0:T(8,128)} %get-tuple-element.12.cb_ref, ...), custom_call_target="tpu_custom_call" | custom-call | tf_op jit(solution)/shard_map/pallas_call | solution.py:94
  75.5 47.6 %shard_map.48 = f32[576,768]{1,0:T(8,128)} custom-call(f32[576,768]{1,0:T(8,128)} %bitcast.16), custom_call_target="tpu_custom_call" | custom-call | tf_op jit(solution)/shard_map/pallas_call | solution.py:191
  123.1 2.6 %reshape.55 = f32[4,4,3,4,3,768]{5,4,3,2,1,0:T(4,128)S(1)} reshape(f32[576,768]{1,0:T(8,128)} %shard_map.48) | data formatting | bytes 3538944 | tf_op jit(solution)/shard_map/reshape | solution.py:324
  125.7 1.7 %copy.32 = f32[4,4,3,4,3,768]{5,3,4,2,1,0:T(4,128)} copy(f32[4,4,3,4,3,768]{5,4,3,2,1,0:T(4,128)S(1)} %reshape.55) | data formatting | bytes 3538944 | tf_op jit(solution)/shard_map/reshape | solution.py:324
  (17 shorter events, 0.4 us)
Async XLA Ops:
  0.0 5.8 %copy-start = (f32[2,4,2,3,1664]{4,2,3,1,0:T(2,128)S(1)}, f32[2,4,2,3,1664]{4,2,3,1,0:T(2,128)}, u32[]{:S(2)}) copy-start(f32[2,4,2,3,1664]{4,2,3,1,0:T(2,128)} %param.4) | copy-start | bytes 958468

commit v15 on v14

--- a/solution.py
+++ b/solution.py
@@ -199,8 +199,8 @@
             pltpu.VMEM((rows // 2, cols), jnp.float32),
             pltpu.VMEM((rows // 4, cols), jnp.float32),
             pltpu.VMEM((rows // 8, cols), jnp.float32),
-            pltpu.SemaphoreType.DMA((18,)),
-            pltpu.SemaphoreType.DMA((18,)),
+            pltpu.SemaphoreType.DMA((36,)),
+            pltpu.SemaphoreType.DMA((36,)),
         ],
         compiler_params=pltpu.CompilerParams(collective_id=0, has_side_effects=True),
     )(x)

time: 128 us -> 133 us (1.039)
  Pallas kernels: 109 us -> 114 us
    pallas_call x1, Pallas kernels: 47.6 us -> 52.2 us  [win_sum(): pl.pallas_call(win_sum_kernel, out_shape=jax.ShapeDtypeStruct((rows, cols...]
where the time goes in v15:
time: 133 us; the launch traced here: 132 us
  Pallas kernels  114 us (86%)
  local copies, waits for them, and re-layouts  10.3 us (8%)
  other arithmetic  7.75 us (6%)
    pallas_call x1, Pallas kernels, bcast(): pl.pallas_call(bcast_kernel, out_shape=jax.ShapeDtypeStruct(shape, jnp.fl...  52.6 us
    pallas_call x1, Pallas kernels, win_sum(): pl.pallas_call(win_sum_kernel, out_shape=jax.ShapeDtypeStruct((rows, cols...  52.2 us
    pallas_call x1, Pallas kernels, correlate_all(): pl.pallas_call(functools.partial(corr_kernel, scale), grid=(steps,), in_s...  8.98 us
    reshape x2, local copies, waits for them, and re-layouts, on_device(): return win_sum(stacked.reshape(-1, NLAG)).reshape(stacked.shape)  4.31 us
    reshape x1, local copies, waits for them, and re-layouts, on_device(): picked_all = bcast(picked_all.reshape(split)).reshape(picked_all.shape)  3 us
    sin x2, other arithmetic, lag_factors(): return (jnp.cos(a), jnp.sin(a), jnp.cos(b), jnp.sin(b))  2.76 us

profile of v15, /device:TPU:1, one launch (start us, length us, event | category | flops | bytes accessed | tf_op | source)
XLA Modules:
  0.0 132.0 jit_solution(7316468417033471824)
XLA Ops:
  0.0 0.7 broadcast_compare_fusion.4
  0.7 0.7 convert_element_type.13
  1.4 0.7 broadcast_compare_fusion.3
  2.1 0.1 copy.19
  2.2 0.1 copy.20
  2.3 0.1 copy.22
  2.4 0.1 copy.23
  2.5 0.1 copy.28
  2.6 0.1 copy.29
  2.7 0.1 copy.25
  2.8 0.1 copy.26
  2.9 1.2 multiply_reduce_fusion
  4.1 0.1 reduce_sum.14
  4.3 0.1 reduce_sum.18
  4.4 0.1 div.21
  4.5 0.1 div.22
  4.6 1.2 fusion.11
  5.8 0.2 divide_multiply_fusion
  6.2 0.2 broadcast_in_dim.124
  6.5 0.2 broadcast_in_dim.131
  6.6 0.1 broadcast_in_dim.137
  6.7 0.2 broadcast_in_dim.138
  7.0 0.2 broadcast_in_dim.117
  7.1 1.4 %select_select_fusion.m_ref = f32[4,8,78,128]{3,2,1,0:T(8,128)} fusion(f32[8,78,128]{2,1,0:T(8,128)S(1)} %broadcast_in_dim.138, f32[8,78,128]{2,1,0:T(8,128)S(1)} %broadcast_in_dim.131, f32[8,78,128]{2,1,0:T(8,128)S(1)} %broadcast_in_dim.124, f32[8,78,128]{2,1,0:T(8,128)S(1)} %broadcast_in_dim.117, pred[4]{0:T(512)(128)(4,1)S(1)} %broadcast_compare_fusion.4, ...), kind=kLoop, calls=%fused_computation | loop fusion | flops 1597440 | bytes 2556036 | tf_op jit(solution)/shard_map/jit(_where)/select_n | solution.py:316
  8.5 52.6 %shard_map.46 = f32[4,8,78,128]{3,2,1,0:T(8,128)} custom-call(f32[4,8,78,128]{3,2,1,0:T(8,128)} %select_select_fusion.m_ref), custom_call_target="tpu_custom_call" | custom-call | tf_op jit(solution)/shard_map/pallas_call | solution.py:280
  61.1 1.6 %fusion.4 = (f32[64,768]{1,0:T(8,128)}, f32[64,768]{1,0:T(8,128)}) fusion(s32[768]{0:T(1024)S(1)} %iota_add_fusion), kind=kLoop, calls=%fused_computation.9 | loop fusion | flops 442368 | bytes 396288 | tf_op jit(solution)/shard_map/sin | solution.py:45
  62.7 3.0 %reshape.53.src_ref = f32[4,2,4,2,3,1664]{5,4,3,2,1,0:T(4,128)} reshape(f32[4,8,78,128]{3,2,1,0:T(8,128)} %shard_map.46) | data formatting | bytes 2555904 | tf_op jit(solution)/shard_map/reshape | solution.py:318
  65.7 0.8 copy.31.rec_ref
  66.5 9.0 %shard_map.47 = f32[4,144,768]{2,1,0:T(8,128)} custom-call(f32[4,2,4,2,3,1664]{5,4,3,2,1,0:T(4,128)} %reshape.53.src_ref, f32[2,2,12,1664]{3,2,1,0:T(8,128)} %copy.31.rec_ref, f32[26,768]{1,0:T(8,128)} %get-tuple-element.10.ca_ref, f32[26,768]{1,0:T(8,128)} %get-tuple-element.9.sa_ref, f32[64,768]{1,0:T(8,128)} %get-tuple-element.12.cb_ref, ...), custom_call_target="tpu_custom_call" | custom-call | tf_op jit(solution)/shard_map/pallas_call | solution.py:94
  75.5 52.2 %shard_map.48 = f32[576,768]{1,0:T(8,128)} custom-call(f32[576,768]{1,0:T(8,128)} %bitcast.16), custom_call_target="tpu_custom_call" | custom-call | tf_op jit(solution)/shard_map/pallas_call | solution.py:191
  127.7 2.6 %reshape.55 = f32[4,4,3,4,3,768]{5,4,3,2,1,0:T(4,128)S(1)} reshape(f32[576,768]{1,0:T(8,128)} %shard_map.48) | data formatting | bytes 3538944 | tf_op jit(solution)/shard_map/reshape | solution.py:324
  130.4 1.7 %copy.32 = f32[4,4,3,4,3,768]{5,3,4,2,1,0:T(4,128)} copy(f32[4,4,3,4,3,768]{5,4,3,2,1,0:T(4,128)S(1)} %reshape.55) | data formatting | bytes 3538944 | tf_op jit(solution)/shard_map/reshape | solution.py:324
  (17 shorter events, 0.4 us)
Async XLA Ops:
  0.0 5.8 %copy-start = (f32[2,4,2,3,1664]{4,2,3,1,0:T(2,128)S(1)}, f32[2,4,2,3,1664]{4,2,3,1,0:T(2,128)}, u32[]{:S(2)}) copy-start(f32[2,4,2,3,1664]{4,2,3,1,0:T(2,128)} %param.4) | copy-start | bytes 958468

commit v16 on v14

--- a/solution.py
+++ b/solution.py
@@ -230,14 +230,22 @@
 
     order = list(range(1, ny)) + [0]
     rs_x = {}
-    for d in order:
+
+    def start_row(i):
+        d = order[i]
         row = (y + d) % ny
         rs_x[d] = [
             remote(m_ref.at[(x + dx) % nx, row], rx.at[x, row], sx, rxs, d * nx + dx, xpeer((x + dx) % nx))
             for dx in range(1, nx)
         ]
+
+    ahead = 2
+    for i in range(min(ahead, ny)):
+        start_row(i)
     rs_y = []
-    for d in order:
+    for i, d in enumerate(order):
+        if i + ahead < ny:
+            start_row(i + ahead)
         row = (y + d) % ny
         for cp in rs_x[d]:
             cp.wait()

time: 128 us -> 127 us (level)
    pallas_call x1, Pallas kernels: 47.6 us -> 45.6 us  [win_sum(): pl.pallas_call(win_sum_kernel, out_shape=jax.ShapeDtypeStruct((rows, cols...]
where the time goes in v16:
time: 127 us; the launch traced here: 126 us
  Pallas kernels  108 us (85%)
  local copies, waits for them, and re-layouts  10.3 us (8%)
  other arithmetic  7.75 us (6%)
    pallas_call x1, Pallas kernels, bcast(): pl.pallas_call(bcast_kernel, out_shape=jax.ShapeDtypeStruct(shape, jnp.fl...  53.5 us
    pallas_call x1, Pallas kernels, win_sum(): pl.pallas_call(win_sum_kernel, out_shape=jax.ShapeDtypeStruct((rows, cols...  45.6 us
    pallas_call x1, Pallas kernels, correlate_all(): pl.pallas_call(functools.partial(corr_kernel, scale), grid=(steps,), in_s...  8.98 us
    reshape x2, local copies, waits for them, and re-layouts, on_device(): return win_sum(stacked.reshape(-1, NLAG)).reshape(stacked.shape)  4.31 us
    reshape x1, local copies, waits for them, and re-layouts, on_device(): picked_all = bcast(picked_all.reshape(split)).reshape(picked_all.shape)  3 us
    sin x2, other arithmetic, lag_factors(): return (jnp.cos(a), jnp.sin(a), jnp.cos(b), jnp.sin(b))  2.76 us

profile of v16, /device:TPU:1, one launch (start us, length us, event | category | flops | bytes accessed | tf_op | source)
XLA Modules:
  0.0 126.3 jit_solution(2905371333641138071)
XLA Ops:
  0.0 0.7 broadcast_compare_fusion.4
  0.7 0.7 convert_element_type.13
  1.4 0.7 broadcast_compare_fusion.3
  2.1 0.1 copy.19
  2.2 0.1 copy.20
  2.3 0.1 copy.22
  2.4 0.1 copy.23
  2.5 0.1 copy.28
  2.6 0.1 copy.29
  2.7 0.1 copy.25
  2.8 0.1 copy.26
  2.9 1.2 multiply_reduce_fusion
  4.1 0.1 reduce_sum.14
  4.3 0.1 reduce_sum.18
  4.4 0.1 div.21
  4.5 0.1 div.22
  4.6 1.2 fusion.11
  5.8 0.2 divide_multiply_fusion
  6.2 0.2 broadcast_in_dim.124
  6.5 0.2 broadcast_in_dim.131
  6.7 0.2 broadcast_in_dim.138
  6.9 0.1 broadcast_in_dim.116
  7.0 0.2 broadcast_in_dim.117
  7.1 1.4 %select_select_fusion.m_ref = f32[4,8,78,128]{3,2,1,0:T(8,128)} fusion(f32[8,78,128]{2,1,0:T(8,128)S(1)} %broadcast_in_dim.138, f32[8,78,128]{2,1,0:T(8,128)S(1)} %broadcast_in_dim.131, f32[8,78,128]{2,1,0:T(8,128)S(1)} %broadcast_in_dim.124, f32[8,78,128]{2,1,0:T(8,128)S(1)} %broadcast_in_dim.117, pred[4]{0:T(512)(128)(4,1)S(1)} %broadcast_compare_fusion.4, ...), kind=kLoop, calls=%fused_computation | loop fusion | flops 1597440 | bytes 2556036 | tf_op jit(solution)/shard_map/jit(_where)/select_n | solution.py:324
  8.5 53.5 %shard_map.46 = f32[4,8,78,128]{3,2,1,0:T(8,128)} custom-call(f32[4,8,78,128]{3,2,1,0:T(8,128)} %select_select_fusion.m_ref), custom_call_target="tpu_custom_call" | custom-call | tf_op jit(solution)/shard_map/pallas_call | solution.py:288
  62.1 1.6 %fusion.4 = (f32[64,768]{1,0:T(8,128)}, f32[64,768]{1,0:T(8,128)}) fusion(s32[768]{0:T(1024)S(1)} %iota_add_fusion), kind=kLoop, calls=%fused_computation.9 | loop fusion | flops 442368 | bytes 396288 | tf_op jit(solution)/shard_map/sin | solution.py:45
  63.6 3.0 %reshape.53.src_ref = f32[4,2,4,2,3,1664]{5,4,3,2,1,0:T(4,128)} reshape(f32[4,8,78,128]{3,2,1,0:T(8,128)} %shard_map.46) | data formatting | bytes 2555904 | tf_op jit(solution)/shard_map/reshape | solution.py:326
  66.7 0.8 copy.31.rec_ref
  67.4 9.0 %shard_map.47 = f32[4,144,768]{2,1,0:T(8,128)} custom-call(f32[4,2,4,2,3,1664]{5,4,3,2,1,0:T(4,128)} %reshape.53.src_ref, f32[2,2,12,1664]{3,2,1,0:T(8,128)} %copy.31.rec_ref, f32[26,768]{1,0:T(8,128)} %get-tuple-element.10.ca_ref, f32[26,768]{1,0:T(8,128)} %get-tuple-element.9.sa_ref, f32[64,768]{1,0:T(8,128)} %get-tuple-element.12.cb_ref, ...), custom_call_target="tpu_custom_call" | custom-call | tf_op jit(solution)/shard_map/pallas_call | solution.py:94
  76.4 45.6 %shard_map.48 = f32[576,768]{1,0:T(8,128)} custom-call(f32[576,768]{1,0:T(8,128)} %bitcast.16), custom_call_target="tpu_custom_call" | custom-call | tf_op jit(solution)/shard_map/pallas_call | solution.py:191
  122.0 2.6 %reshape.55 = f32[4,4,3,4,3,768]{5,4,3,2,1,0:T(4,128)S(1)} reshape(f32[576,768]{1,0:T(8,128)} %shard_map.48) | data formatting | bytes 3538944 | tf_op jit(solution)/shard_map/reshape | solution.py:332
  124.7 1.7 %copy.32 = f32[4,4,3,4,3,768]{5,3,4,2,1,0:T(4,128)} copy(f32[4,4,3,4,3,768]{5,4,3,2,1,0:T(4,128)S(1)} %reshape.55) | data formatting | bytes 3538944 | tf_op jit(solution)/shard_map/reshape | solution.py:332
  (17 shorter events, 0.4 us)
Async XLA Ops:
  0.0 5.8 %copy-start = (f32[2,4,2,3,1664]{4,2,3,1,0:T(2,128)S(1)}, f32[2,4,2,3,1664]{4,2,3,1,0:T(2,128)}, u32[]{:S(2)}) copy-start(f32[2,4,2,3,1664]{4,2,3,1,0:T(2,128)} %param.4) | copy-start | bytes 958468

commit v17 on v16

--- a/solution.py
+++ b/solution.py
@@ -239,7 +239,7 @@
             for dx in range(1, nx)
         ]
 
-    ahead = 2
+    ahead = 1
     for i in range(min(ahead, ny)):
         start_row(i)
     rs_y = []

time: 127 us -> 129 us (1.016)
  Pallas kernels: 108 us -> 111 us
    pallas_call x1, Pallas kernels: 53.5 us -> 58 us  [bcast(): pl.pallas_call(bcast_kernel, out_shape=jax.ShapeDtypeStruct(shape, jnp.fl...]
    pallas_call x1, Pallas kernels: 45.6 us -> 43.8 us  [win_sum(): pl.pallas_call(win_sum_kernel, out_shape=jax.ShapeDtypeStruct((rows, cols...]
where the time goes in v17:
time: 129 us
  Pallas kernels  111 us (86%)
  local copies, waits for them, and re-layouts  10.3 us (8%)
  other arithmetic  7.75 us (6%)
    pallas_call x1, Pallas kernels, bcast(): pl.pallas_call(bcast_kernel, out_shape=jax.ShapeDtypeStruct(shape, jnp.fl...  58 us
    pallas_call x1, Pallas kernels, win_sum(): pl.pallas_call(win_sum_kernel, out_shape=jax.ShapeDtypeStruct((rows, cols...  43.8 us
    pallas_call x1, Pallas kernels, correlate_all(): pl.pallas_call(functools.partial(corr_kernel, scale), grid=(steps,), in_s...  8.98 us
    reshape x2, local copies, waits for them, and re-layouts, on_device(): return win_sum(stacked.reshape(-1, NLAG)).reshape(stacked.shape)  4.31 us
    reshape x1, local copies, waits for them, and re-layouts, on_device(): picked_all = bcast(picked_all.reshape(split)).reshape(picked_all.shape)  3 us
    sin x2, other arithmetic, lag_factors(): return (jnp.cos(a), jnp.sin(a), jnp.cos(b), jnp.sin(b))  2.76 us

profile of v17, /device:TPU:1, one launch (start us, length us, event | category | flops | bytes accessed | tf_op | source)
XLA Modules:
  0.0 129.0 jit_solution(7032602509238853161)
XLA Ops:
  0.0 0.7 broadcast_compare_fusion.4
  0.7 0.7 convert_element_type.13
  1.4 0.7 broadcast_compare_fusion.3
  2.1 0.1 copy.19
  2.2 0.1 copy.20
  2.3 0.1 copy.22
  2.4 0.1 copy.23
  2.5 0.1 copy.28
  2.6 0.1 copy.29
  2.7 0.1 copy.25
  2.8 0.1 copy.26
  2.9 1.2 multiply_reduce_fusion
  4.1 0.1 reduce_sum.14
  4.3 0.1 reduce_sum.18
  4.4 0.1 div.21
  4.5 0.1 div.22
  4.6 1.2 fusion.11
  5.8 0.2 divide_multiply_fusion
  6.2 0.2 broadcast_in_dim.124
  6.5 0.2 broadcast_in_dim.131
  6.6 0.1 broadcast_in_dim.137
  6.7 0.2 broadcast_in_dim.138
  7.0 0.2 broadcast_in_dim.117
  7.1 1.4 %select_select_fusion.m_ref = f32[4,8,78,128]{3,2,1,0:T(8,128)} fusion(f32[8,78,128]{2,1,0:T(8,128)S(1)} %broadcast_in_dim.138, f32[8,78,128]{2,1,0:T(8,128)S(1)} %broadcast_in_dim.131, f32[8,78,128]{2,1,0:T(8,128)S(1)} %broadcast_in_dim.124, f32[8,78,128]{2,1,0:T(8,128)S(1)} %broadcast_in_dim.117, pred[4]{0:T(512)(128)(4,1)S(1)} %broadcast_compare_fusion.4, ...), kind=kLoop, calls=%fused_computation | loop fusion | flops 1597440 | bytes 2556036 | tf_op jit(solution)/shard_map/jit(_where)/select_n | solution.py:324
  8.5 58.0 %shard_map.46 = f32[4,8,78,128]{3,2,1,0:T(8,128)} custom-call(f32[4,8,78,128]{3,2,1,0:T(8,128)} %select_select_fusion.m_ref), custom_call_target="tpu_custom_call" | custom-call | tf_op jit(solution)/shard_map/pallas_call | solution.py:288
  66.5 1.6 %fusion.4 = (f32[64,768]{1,0:T(8,128)}, f32[64,768]{1,0:T(8,128)}) fusion(s32[768]{0:T(1024)S(1)} %iota_add_fusion), kind=kLoop, calls=%fused_computation.9 | loop fusion | flops 442368 | bytes 396288 | tf_op jit(solution)/shard_map/sin | solution.py:45
  68.1 3.0 %reshape.53.src_ref = f32[4,2,4,2,3,1664]{5,4,3,2,1,0:T(4,128)} reshape(f32[4,8,78,128]{3,2,1,0:T(8,128)} %shard_map.46) | data formatting | bytes 2555904 | tf_op jit(solution)/shard_map/reshape | solution.py:326
  71.1 0.8 copy.31.rec_ref
  71.9 9.0 %shard_map.47 = f32[4,144,768]{2,1,0:T(8,128)} custom-call(f32[4,2,4,2,3,1664]{5,4,3,2,1,0:T(4,128)} %reshape.53.src_ref, f32[2,2,12,1664]{3,2,1,0:T(8,128)} %copy.31.rec_ref, f32[26,768]{1,0:T(8,128)} %get-tuple-element.10.ca_ref, f32[26,768]{1,0:T(8,128)} %get-tuple-element.9.sa_ref, f32[64,768]{1,0:T(8,128)} %get-tuple-element.12.cb_ref, ...), custom_call_target="tpu_custom_call" | custom-call | tf_op jit(solution)/shard_map/pallas_call | solution.py:94
  80.9 43.8 %shard_map.48 = f32[576,768]{1,0:T(8,128)} custom-call(f32[576,768]{1,0:T(8,128)} %bitcast.16), custom_call_target="tpu_custom_call" | custom-call | tf_op jit(solution)/shard_map/pallas_call | solution.py:191
  124.7 2.6 %reshape.55 = f32[4,4,3,4,3,768]{5,4,3,2,1,0:T(4,128)S(1)} reshape(f32[576,768]{1,0:T(8,128)} %shard_map.48) | data formatting | bytes 3538944 | tf_op jit(solution)/shard_map/reshape | solution.py:332
  127.3 1.7 %copy.32 = f32[4,4,3,4,3,768]{5,3,4,2,1,0:T(4,128)} copy(f32[4,4,3,4,3,768]{5,4,3,2,1,0:T(4,128)S(1)} %reshape.55) | data formatting | bytes 3538944 | tf_op jit(solution)/shard_map/reshape | solution.py:332
  (17 shorter events, 0.4 us)
Async XLA Ops:
  0.0 5.8 %copy-start = (f32[2,4,2,3,1664]{4,2,3,1,0:T(2,128)S(1)}, f32[2,4,2,3,1664]{4,2,3,1,0:T(2,128)}, u32[]{:S(2)}) copy-start(f32[2,4,2,3,1664]{4,2,3,1,0:T(2,128)} %param.4) | copy-start | bytes 958468
